TPU v7x, 256 devices: a whole 4x4x8 slice. The times are simulated.
256 devices in a mesh: pole: 8 (over x, core), rows: 32 (over z, y).
Axes of the slice: x: 4, y: 4, z: 8, core: 2. Of those that a mesh axis runs over, the one named last changes fastest.
Arguments:
- subspace: float32 [2, 256, 16384], P(None, None, 'rows'), may hold values from -6 to 6
- pivots: float32 [8, 64, 2, 256, 256], P('pole', 'rows'), may hold values from -0.25 to 0.25
- lower_blocks: float32 [8, 64, 2, 256, 256], P('pole', 'rows'), may hold values from -1 to 1
- upper_blocks: float32 [8, 64, 2, 256, 256], P('pole', 'rows'), may hold values from -1 to 1
- pole_weights: float32 [8, 2], P('pole'), may hold values from -4 to 4
Outputs:
- rotated_basis: float32 [2, 256, 16384], P(None, 'pole', 'rows')
All inputs are finite; a program needn't handle non-finite values.
Results may differ from a plain program's by a relative error of at most 0.00018.
Values sent between devices are 32-bit elements; how exact they have to be, the bound alone decides.
A program may use at most 128 MiB of HBM per device.

v0:
```python
import jax
import jax.numpy as jnp
from jax import lax
from jax.sharding import Mesh
from jax.sharding import PartitionSpec as P

NS_ITERS = 2
ROWS = ("rows_0", "rows_1")


HIGH = lax.Precision.HIGHEST


def neutral_like(array, identity):
    return jax.tree.map(
        lambda a, e: jnp.broadcast_to(jnp.asarray(e, a.dtype), a.shape), array, identity
    )


def prefix_by_axis(array, axes, combine, identity, reverse):
    before = start = neutral_like(array, identity)
    so_far = array
    for axis in reversed(axes):
        count, place = (lax.axis_size(axis), lax.axis_index(axis))
        pieces = jax.tree.map(lambda part: lax.all_gather(part, axis), so_far)
        inside, so_far = (start, start)
        for k in reversed(range(count)) if reverse else range(count):
            passed = k > place if reverse else k < place
            so_far = combine(so_far, jax.tree.map(lambda part: part[k], pieces))
            inside = jax.tree.map(lambda new, old: jnp.where(passed, new, old), so_far, inside)
        before = combine(inside, before)
    return before


def over_pieces(array, axis):
    blocks = lax.all_gather(array, axis)
    return blocks.sum(axis=0)


def rows_for(lines, count):
    spare = -lines.shape[0] % count
    if not spare:
        return lines
    return jnp.concatenate([lines, jnp.zeros((spare, *lines.shape[1:]), lines.dtype)])


def reduced_to_own(blocks, axes, turns):
    dims = [lax.axis_size(a) for a in axes]
    blocks = blocks.reshape(*dims, *blocks.shape[1:])
    blocks = blocks.transpose(*turns, *range(len(axes), blocks.ndim))
    blocks = blocks.reshape(-1, *blocks.shape[len(axes) :])
    for k in turns:
        blocks = lax.psum_scatter(blocks, axes[k], scatter_dimension=0, tiled=True)
    return blocks[0]


def stacked_from(array, axes, turns):
    blocks = array[None]
    for k in turns:
        blocks = lax.all_gather(blocks, axes[k], axis=0, tiled=True)
    block = [lax.axis_size(axes[k]) for k in reversed(turns)]
    blocks = blocks.reshape(*block, *array.shape)
    turned = sorted(range(len(turns)), key=lambda place: turns[len(turns) - 1 - place])
    return blocks.transpose(*turned, *range(len(turns), blocks.ndim)).reshape(-1, *array.shape)


def total_of(array, axes, turns):
    count, lines = (lax.axis_size(axes), array.reshape(-1, *array.shape[1:][-1:]))
    blocks = rows_for(lines, count).reshape(count, -1, *lines.shape[1:])
    own = reduced_to_own(blocks, axes, turns)
    whole = stacked_from(own, axes, turns[::-1]).reshape(-1, *lines.shape[1:])
    return whole[: len(lines)].reshape(array.shape)


def real_dot(first, second, dims):
    return lax.dot_general(
        first, second, (dims, ((), ())), precision=HIGH, preferred_element_type=jnp.float32
    )


def times_trans(left, matrix):
    dims = ((1,), (1,))
    real = real_dot(left[0], matrix[0], dims) - real_dot(left[1], matrix[1], dims)
    imag = real_dot(left[0], matrix[1], dims) + real_dot(left[1], matrix[0], dims)
    return jnp.stack([real, imag])


def complex_dot(left, right):
    dims = ((1,), (0,))
    real = real_dot(left[0], right[0], dims) - real_dot(left[1], right[1], dims)
    imag = real_dot(left[0], right[1], dims) + real_dot(left[1], right[0], dims)
    return jnp.stack([real, imag])


def gram_matrix(basis):
    dims = ((1,), (1,))
    real = real_dot(basis[0], basis[0], dims) + real_dot(basis[1], basis[1], dims)
    imag = real_dot(basis[0], basis[1], dims) - real_dot(basis[1], basis[0], dims)
    return jnp.stack([real, imag])


def rotate(mixing, basis):
    dims = ((0,), (0,))
    real = real_dot(mixing[0], basis[0], dims) - real_dot(mixing[1], basis[1], dims)
    imag = real_dot(mixing[0], basis[1], dims) + real_dot(mixing[1], basis[0], dims)
    return jnp.stack([real, imag])


def unit_matrix(size):
    return jnp.stack([jnp.eye(size, dtype=jnp.float32), jnp.zeros((size, size), jnp.float32)])


def newton_schulz(gram):
    unit = unit_matrix(gram.shape[1])
    frob = jnp.sqrt(jnp.sum(gram * gram))
    current = gram / frob
    inverse_root = unit
    for sweep in range(NS_ITERS):
        scale_factor = 1.5 * unit - 0.5 * complex_dot(inverse_root, current)
        current = complex_dot(current, scale_factor)
        inverse_root = complex_dot(scale_factor, inverse_root)
    return (inverse_root, frob)


def chain(earlier, later):
    return (complex_dot(earlier[0], later[0]), complex_dot(earlier[1], later[0]) + later[1])


def shards(subspace, pivots, lower_blocks, upper_blocks, pole_weights):
    width = pivots.shape[-1]
    count = pivots.shape[1]
    vectors = subspace.shape[1]
    pivot = pivots[0]
    lower = lower_blocks[0]
    upper = upper_blocks[0]
    pieces = subspace.reshape(2, vectors, count, width)
    unit = unit_matrix(width)
    blank = jnp.zeros((2, vectors, width), jnp.float32)
    forward = []
    carried = []
    for number in range(count):
        summand = times_trans(pieces[:, :, number, :], pivot[number])
        if number == 0:
            passing = -jnp.swapaxes(lower[0], 1, 2)
        else:
            summand = summand - times_trans(forward[-1], lower[number])
            passing = -times_trans(passing, lower[number])
        forward.append(summand)
        carried.append(passing)
    _, inflow = prefix_by_axis((carried[-1], forward[-1]), ROWS, chain, (unit, blank), False)
    swept = [forward[number] + complex_dot(inflow, carried[number]) for number in range(count)]
    backward = [None] * count
    reaches = [None] * count
    backward[count - 1] = swept[count - 1]
    reaches[count - 1] = -jnp.swapaxes(upper[count - 1], 1, 2)
    number = 0
    backward[number] = swept[number] - times_trans(backward[number + 1], upper[number])
    reaches[number] = -times_trans(reaches[number + 1], upper[number])
    _, outflow = prefix_by_axis((reaches[0], backward[0]), ROWS, chain, (unit, blank), True)
    solved = [backward[number] + complex_dot(outflow, reaches[number]) for number in range(count)]
    solution = jnp.stack(solved, axis=2).reshape(2, vectors, count * width)
    wreal = pole_weights[0, 0]
    wimag = pole_weights[0, 1]
    weighted = jnp.stack(
        [wreal * solution[0] - wimag * solution[1], wreal * solution[1] + wimag * solution[0]]
    )
    total_rows = count * width * lax.axis_size(ROWS)
    summed = over_pieces(weighted, "pole")
    gram = total_of(gram_matrix(summed), ROWS, (0, 1))
    inverse_root, frob = newton_schulz(gram)
    columns = vectors // lax.axis_size("pole")
    mixing = lax.dynamic_slice_in_dim(inverse_root, lax.axis_index("pole") * columns, columns, 2)
    result = rotate(mixing, summed) * jnp.sqrt(total_rows / frob)
    return result


def solution(mesh):
    torus = Mesh(mesh.devices.reshape(mesh.shape["pole"], 8, 4), ("pole", "rows_0", "rows_1"))
    return jax.shard_map(
        shards,
        mesh=torus,
        in_specs=(
            P(None, None, ROWS),
            P("pole", ROWS, None, None, None),
            P("pole", ROWS, None, None, None),
            P("pole", ROWS, None, None, None),
            P("pole", None),
        ),
        out_specs=P(None, "pole", ROWS),
        check_vma=False,
    )
```

profile of v0, /device:TPU:2, one launch (start us, length us, event | category | flops | bytes accessed | tf_op | source)
XLA Modules:
  0.0 667.6 jit_solution(13590297586128555691)
XLA Ops:
  7.6 1.5 fusion.147
  9.2 1.6 fusion.140
  10.8 1.5 convolution_subtract_fusion.47
  12.4 1.6 convolution_add_fusion.47
  15.0 2.9 reshape.693
  17.9 2.6 fusion.284
  31.7 19.7 %all-gather.13.cloned.1.call-done = f32[4,2,256,256]{3,2,1,0:T(8,128)} async-done(((f32[1,2,256,256]{3,2,1,0:T(8,128)}), f32[4,2,256,256]{3,2,1,0:T(8,128)}) %all-gather.13.cloned.1.call-update) | async-done | bytes 2097168 | tf_op jit(solution)/shard_map/all_gather | solution.py:25
  63.9 22.8 %all-gather.15.cloned.1.call-done = f32[4,2,256,256]{3,2,1,0:T(8,128)} async-done(((f32[1,2,256,256]{3,2,1,0:T(8,128)}), f32[4,2,256,256]{3,2,1,0:T(8,128)}) %all-gather.15.cloned.1.call-update) | async-done | bytes 2097168 | tf_op jit(solution)/shard_map/all_gather | solution.py:25
  86.8 1.3 fusion.92
  96.0 26.0 %all-gather.19.cloned.1.call-done = f32[4,2,256,256]{3,2,1,0:T(8,128)} async-done(((f32[1,2,256,256]{3,2,1,0:T(8,128)}), f32[4,2,256,256]{3,2,1,0:T(8,128)}) %all-gather.19.cloned.1.call-update) | async-done | bytes 2097168 | tf_op jit(solution)/shard_map/all_gather | solution.py:25
  123.1 2.4 fusion.95
  129.5 49.1 %all-gather.25.cloned.1.call-done = f32[16,256,256]{2,1,0:T(8,128)} async-done(((f32[2,256,256]{2,1,0:T(8,128)}), f32[16,256,256]{2,1,0:T(8,128)}) %all-gather.25.cloned.1.call-update) | async-done | bytes 4194320 | tf_op jit(solution)/shard_map/all_gather | solution.py:25
  179.6 54.0 %all-gather.17.cloned.1.call-done = f32[8,2,256,256]{3,2,1,0:T(8,128)} async-done(((f32[1,2,256,256]{3,2,1,0:T(8,128)}), f32[8,2,256,256]{3,2,1,0:T(8,128)}) %all-gather.17.cloned.1.call-update) | async-done | bytes 4194320 | tf_op jit(solution)/shard_map/all_gather | solution.py:25
  237.5 1.3 fusion.51
  263.4 1.3 fusion.43
  268.5 1.5 fusion.174
  271.3 1.8 fusion.40
  276.9 1.3 fusion.39
  296.4 25.5 %all-gather.21.cloned.1.call-done = f32[4,2,256,256]{3,2,1,0:T(8,128)} async-done(((f32[1,2,256,256]{3,2,1,0:T(8,128)}), f32[4,2,256,256]{3,2,1,0:T(8,128)}) %all-gather.21.cloned.1.call-update) | async-done | bytes 2097168 | tf_op jit(solution)/shard_map/all_gather | solution.py:25
  322.0 1.3 fusion.80
  337.0 41.6 %all-gather.27.cloned.1.call-done = f32[16,256,256]{2,1,0:T(8,128)} async-done(((f32[2,256,256]{2,1,0:T(8,128)}), f32[16,256,256]{2,1,0:T(8,128)}) %all-gather.27.cloned.1.call-update) | async-done | bytes 4194320 | tf_op jit(solution)/shard_map/all_gather | solution.py:25
  379.7 2.1 fusion.98
  384.5 49.3 %all-gather.23.cloned.1.call-done = f32[8,2,256,256]{3,2,1,0:T(8,128)} async-done(((f32[1,2,256,256]{3,2,1,0:T(8,128)}), f32[8,2,256,256]{3,2,1,0:T(8,128)}) %all-gather.23.cloned.1.call-update) | async-done | bytes 4194320 | tf_op jit(solution)/shard_map/all_gather | solution.py:25
  468.7 1.5 fusion.200
  471.5 1.7 fusion.16
  486.6 1.5 multiply_subtract_fusion
  489.6 50.2 %all-gather.29.cloned.1.call-done = f32[16,256,512]{2,1,0:T(8,128)} async-done(((f32[2,256,512]{2,1,0:T(8,128)}), f32[16,256,512]{2,1,0:T(8,128)}) %all-gather.29.cloned.1.call-update) | async-done | bytes 8388624 | tf_op jit(solution)/shard_map/all_gather | solution.py:36
  539.8 4.5 reduce_sum.18
  547.7 38.3 %reduce-scatter.3.cloned.1.call-done = f32[4,16,256]{2,1,0:T(8,128)} async-done(((f32[32,16,256]{2,1,0:T(8,128)}), f32[4,16,256]{2,1,0:T(8,128)}) %reduce-scatter.3.cloned.1.call-update) | async-done | bytes 65552 | tf_op jit(solution)/shard_map/reduce_scatter | solution.py:53
  586.1 24.1 %reduce-scatter.5.cloned.1.call-done = f32[1,16,256]{2,1,0:T(8,128)} async-done(((f32[4,16,256]{2,1,0:T(8,128)}), f32[1,16,256]{2,1,0:T(8,128)}) %reduce-scatter.5.cloned.1.call-update) | async-done | bytes 16400 | tf_op jit(solution)/shard_map/reduce_scatter | solution.py:53
  610.3 12.1 %all_gather.60 = f32[4,16,256]{2,1,0:T(8,128)S(1)} all-gather(f32[1,16,256]{2,1,0:T(8,128)} %reduce-scatter.5.cloned.1.call-done), channel_id=1, replica_groups=mesh['pole'=8,'rows_0'=8,'rows_1'=4] {'rows_1'}, dimensions={0}, use_global_device_ids=true | all-gather | bytes 81920 | tf_op jit(solution)/shard_map/all_gather | solution.py:60
  622.3 27.0 %all_gather.61 = f32[32,16,256]{2,1,0:T(8,128)S(1)} all-gather(f32[4,16,256]{2,1,0:T(8,128)S(1)} %all_gather.60), channel_id=1, replica_groups=mesh['pole'=8,'rows_0'=8,'rows_1'=4] {'rows_0'}, dimensions={0}, use_global_device_ids=true | all-gather | bytes 589824 | tf_op jit(solution)/shard_map/all_gather | solution.py:60
  (414 shorter events, 175.5 us)
Async XLA Ops:
  6.5 44.9 %all-gather.13.cloned.1.call-start = ((), (), s32[]{:S(2)}) async-start(), calls=%async_computation.2 | async-start | bytes 2621440 | tf_op jit(solution)/shard_map/all_gather | solution.py:25
  9.2 11.3 %copy-start.13 = (f32[1,2,2,256,256]{4,3,2,1,0:T(8,128)S(1)}, f32[1,2,2,256,256]{4,3,2,1,0:T(8,128)}, u32[]{:S(2)}) copy-start(f32[1,2,2,256,256]{4,3,2,1,0:T(8,128)} %param.6) | copy-start | bytes 3145732
  14.0 7.7 %copy-start.6 = (f32[1,2,2,256,256]{4,3,2,1,0:T(8,128)S(1)}, f32[1,2,2,256,256]{4,3,2,1,0:T(8,128)}, u32[]{:S(2)}) copy-start(f32[1,2,2,256,256]{4,3,2,1,0:T(8,128)} %param.7) | copy-start | bytes 3145732
  14.9 71.8 %all-gather.15.cloned.1.call-start = ((), (), s32[]{:S(2)}) async-start(), calls=%async_computation.3 | async-start | bytes 2621440 | tf_op jit(solution)/shard_map/all_gather | solution.py:25
  17.9 5.5 copy-start.14
  27.4 94.6 %all-gather.19.cloned.1.call-start = ((), (), s32[]{:S(2)}) async-start(), calls=%async_computation.5 | async-start | bytes 2621440 | tf_op jit(solution)/shard_map/all_gather | solution.py:25
  31.6 146.9 %all-gather.25.cloned.1.call-start = ((), (), s32[]{:S(2)}) async-start(), calls=%async_computation.10 | async-start | bytes 4718592 | tf_op jit(solution)/shard_map/all_gather | solution.py:25
  51.4 7.8 %copy-start.1 = (f32[4,2,256,256]{3,2,1,0:T(8,128)S(1)}, f32[4,2,256,256]{3,2,1,0:T(8,128)}, u32[]{:S(2)}) copy-start(f32[4,2,256,256]{3,2,1,0:T(8,128)} %all-gather.13.cloned.1.call-done) | copy-start | bytes 6291460
  63.8 169.8 %all-gather.17.cloned.1.call-start = ((), (), s32[]{:S(2)}) async-start(), calls=%async_computation.4 | async-start | bytes 4718592 | tf_op jit(solution)/shard_map/all_gather | solution.py:25
  94.7 227.2 %all-gather.21.cloned.1.call-start = ((), (), s32[]{:S(2)}) async-start(), calls=%async_computation.6 | async-start | bytes 2621440 | tf_op jit(solution)/shard_map/all_gather | solution.py:25
  96.0 32.2 %copy-start.12 = (f32[2,256,256]{2,1,0:T(8,128)S(1)}, f32[2,256,256]{2,1,0:T(8,128)}, u32[]{:S(2)}) copy-start(f32[2,256,256]{2,1,0:T(8,128)} %get-tuple-element.24) | copy-start | bytes 1572868
  268.5 11.1 %copy-start.2 = (f32[8,2,256,256]{3,2,1,0:T(8,128)S(1)}, f32[8,2,256,256]{3,2,1,0:T(8,128)}, u32[]{:S(2)}) copy-start(f32[8,2,256,256]{3,2,1,0:T(8,128)} %all-gather.17.cloned.1.call-done) | copy-start | bytes 12582916
  289.7 88.8 %all-gather.27.cloned.1.call-start = ((), (), s32[]{:S(2)}) async-start(), calls=%async_computation.11 | async-start | bytes 4718592 | tf_op jit(solution)/shard_map/all_gather | solution.py:25
  296.4 137.5 %all-gather.23.cloned.1.call-start = ((), (), s32[]{:S(2)}) async-start(), calls=%async_computation.7 | async-start | bytes 4718592 | tf_op jit(solution)/shard_map/all_gather | solution.py:25
  328.3 51.4 %copy-start.33 = (f32[1,256,256]{2,1,0:T(8,128)S(1)}, f32[1,256,256]{2,1,0:T(8,128)}, u32[]{:S(2)}) copy-start(f32[1,256,256]{2,1,0:T(8,128)} %copy-done.32) | copy-start | bytes 786436
  328.3 51.4 %copy-start.35 = (f32[1,256,256]{2,1,0:T(8,128)S(1)}, f32[1,256,256]{2,1,0:T(8,128)}, u32[]{:S(2)}) copy-start(f32[1,256,256]{2,1,0:T(8,128)} %copy-done.34) | copy-start | bytes 786436
  328.9 50.7 %copy-start.37 = (f32[1,256,256]{2,1,0:T(8,128)S(1)}, f32[1,256,256]{2,1,0:T(8,128)}, u32[]{:S(2)}) copy-start(f32[1,256,256]{2,1,0:T(8,128)} %copy-done.36) | copy-start | bytes 786436
  329.8 49.9 %copy-start.39 = (f32[256,256]{1,0:T(8,128)S(1)}, f32[256,256]{1,0:T(8,128)}, u32[]{:S(2)}) copy-start(f32[256,256]{1,0:T(8,128)} %copy-done.38) | copy-start | bytes 786436
  329.8 209.9 %all-gather.29.cloned.1.call-start = ((), (), s32[]{:S(2)}) async-start(), calls=%async_computation.12 | async-start | bytes 9437184 | tf_op jit(solution)/shard_map/all_gather | solution.py:36
  468.7 11.1 %copy-start.3 = (f32[8,2,256,256]{3,2,1,0:T(8,128)S(1)}, f32[8,2,256,256]{3,2,1,0:T(8,128)}, u32[]{:S(2)}) copy-start(f32[8,2,256,256]{3,2,1,0:T(8,128)} %all-gather.23.cloned.1.call-done) | copy-start | bytes 12582916
  481.9 4.3 copy-start.11
  481.9 4.3 copy-start.17
  481.9 4.3 copy-start.20
  481.9 4.3 copy-start.23
  481.9 4.3 copy-start.26
  481.9 4.3 copy-start.50
  481.9 4.3 copy-start.52
  482.0 4.3 copy-start.54
  482.0 4.3 copy-start.56
  482.0 4.3 copy-start.58
  489.6 96.5 %reduce-scatter.3.cloned.1.call-start = ((), (), s32[]{:S(2)}) async-start(), calls=%async_computation.8 | async-start | bytes 589824 | tf_op jit(solution)/shard_map/reduce_scatter | solution.py:53
  547.7 62.6 %reduce-scatter.5.cloned.1.call-start = ((), (), s32[]{:S(2)}) async-start(), calls=%async_computation.9 | async-start | bytes 81920 | tf_op jit(solution)/shard_map/reduce_scatter | solution.py:53
  (47 other events, 110.2 us)
Sparse Core Ops, SparseCore 0:
  15.0 36.3 all-gather.12
  53.2 33.4 all-gather.14
  88.5 33.4 all-gather.18
  123.7 54.8 all-gather.24
  180.2 53.4 all-gather.16
  289.8 32.0 all-gather.20
  323.7 54.8 all-gather.26
  380.4 53.4 all-gather.22
  489.7 50.0 all-gather.28
  547.8 38.2 reduce-scatter.2
  588.7 21.4 reduce-scatter.4
where the time goes:
time: 678 us; the launch traced here: 668 us
  waiting for transfers between devices  401 us (59%)
  matrix products  149 us (22%)
  other arithmetic  47.9 us (7%)
  blocking collectives  39 us (6%)
  between operations  17 us (3%)
  local copies, waits for them, and re-layouts  12.5 us (2%)
    all_gather x8, waiting for transfers between devices, prefix_by_axis(): pieces = jax.tree.map(lambda part: lax.all_gather(part, axis), so_far)  288 us
    dot_general x198, matrix products, real_dot(): lax.dot_general(first, second, (dims, ((), ())), precision=HIGH, preferre...  149 us
    reduce_scatter x2, waiting for transfers between devices, reduced_to_own(): blocks = lax.psum_scatter(blocks, axes[k], scatter_dimension=0, tiled=True)  62.5 us
    all_gather x1, waiting for transfers between devices, over_pieces(): blocks = lax.all_gather(array, axis)  50.2 us
    all_gather x2, blocking collectives, stacked_from(): blocks = lax.all_gather(blocks, axes[k], axis=0, tiled=True)  39 us
    add x24, other arithmetic, chain(): complex_dot(earlier[1], later[0]) + later[1]  20.4 us
  transfers between devices with their start and end apart: 11, of which 11 were waited for; matrix products, arithmetic and copies ran while one was open for 10% of the time, Pallas kernels for 0%

commit v1 on v0

v1 whole, which is shorter than its diff:
```python
import functools

import jax
import jax.numpy as jnp
from jax import lax
from jax.experimental import pallas as pl
from jax.experimental.pallas import tpu as pltpu
from jax.sharding import Mesh
from jax.sharding import PartitionSpec as P

F32 = jnp.float32
BF16 = jnp.bfloat16
MESH_ID = pl.DeviceIdType.MESH
AXES = ("x", "core", "z", "y")
SUBS = 4


def halves(value):
    high = value.astype(BF16)
    return high, (value - high.astype(F32)).astype(BF16)


def dot(left, right, trans):
    dims = (((1,), (1 if trans else 0,)), ((), ()))
    return lax.dot_general(left, right, dims, preferred_element_type=F32)


def times(rows, weights, trans):
    high, low = halves(rows)
    count = rows.shape[0]
    both = dot(jnp.concatenate([high, low], axis=0), weights[0], trans)
    return both[:count] + both[count:] + dot(high, weights[1], trans)


def prepare(weights, real, minus):
    size = real.shape[0]
    for part, (r, m) in enumerate(zip(halves(real), halves(minus))):
        weights[part, :size, :size] = r
        weights[part, :size, size:] = m
        weights[part, size:, :size] = -m
        weights[part, size:, size:] = r


def tiles(count, size, body):
    if count == size:
        body(0)
        return

    def step(i, carry):
        body(pl.multiple_of(i * size, size))
        return carry

    lax.fori_loop(0, count // size, step, 0)


def remote(src, dst, sems, slot_out, slot_in, device):
    return pltpu.make_async_remote_copy(
        src_ref=src,
        dst_ref=dst,
        send_sem=sems.at[0, slot_out],
        recv_sem=sems.at[1, slot_in],
        device_id=device,
        device_id_type=MESH_ID,
    )


def nearest_first(count):
    return sorted(range(1, count), key=lambda d: min(d, count - d))


def sweeps(
    dims, f_ref, g_ref, e_ref, u_ref, w_ref, out_ref,
    we0, we1, wf0, wf1, wg, wc, wd, wp, wq,
    c_all, d_all, b_all, e_all, qg, rg, s0, s1, y0, y1, eo, vin, win,
    vz, vo, wz, wo, vk, wk,
    sem_c, sem_b, sem_d, sem_v, sem_e, sem_w, sem_fz, sem_bz,
):
    ysize, zsize = dims
    y, z = lax.axis_index("y"), lax.axis_index("z")
    vectors, width = f_ref.shape[1], g_ref.shape[-1]
    chunk = vectors // ysize
    sub = chunk // SUBS
    tall = min(128, width)
    order = nearest_first(ysize)

    barrier = pltpu.get_barrier_semaphore()
    for d in order:
        pl.semaphore_signal(barrier, inc=1, device_id={"y": lax.rem(y + d, ysize)}, device_id_type=MESH_ID)
    for d in (1, zsize - 1):
        pl.semaphore_signal(barrier, inc=1, device_id={"z": lax.rem(z + d, zsize)}, device_id_type=MESH_ID)
    pl.semaphore_wait(barrier, ysize + 1)

    def piece(ref, j):
        return ref.at[pl.ds(pl.multiple_of(j * chunk, chunk), chunk), :]

    def to_all(store, sems):
        sent = []
        for d in order:
            copy = remote(store.at[y], store.at[y], sems, d, d, {"y": lax.rem(y + d, ysize)})
            copy.start()
            sent.append(copy)
        return sent

    def to_each(source, store, sems, d):
        peer = lax.rem(y + d, ysize)
        copy = remote(piece(source, peer), store, sems, d, d, {"y": peer})
        copy.start()
        return copy

    def arrived(store, sems, d):
        remote(store, store, sems, d, d, {"y": lax.rem(y + ysize - d, ysize)}).wait_recv()

    sent = []

    prepare(we0, e_ref[0, 0, 0], -e_ref[0, 0, 1])

    def forward_map(i):
        rows = jnp.concatenate([e_ref[0, 1, 0, pl.ds(i, tall), :], -e_ref[0, 1, 1, pl.ds(i, tall), :]], axis=1)
        c_all[y, pl.ds(i, tall), :] = times(rows, we0, False)

    tiles(width, tall, forward_map)
    sent += to_all(c_all, sem_c)

    prepare(wg.at[0], g_ref[0, 0, 0], -g_ref[0, 0, 1])
    prepare(wg.at[1], g_ref[0, 1, 0], -g_ref[0, 1, 1])
    prepare(we1, e_ref[0, 1, 0], -e_ref[0, 1, 1])

    def local(i):
        rows = pl.ds(i, tall)
        first = jnp.concatenate([f_ref[0, rows, :width], f_ref[1, rows, :width]], axis=1)
        second = jnp.concatenate([f_ref[0, rows, width:], f_ref[1, rows, width:]], axis=1)
        start = times(first, wg.at[0], True)
        s0[rows, :] = start
        s1[rows, :] = times(second, wg.at[1], True) - times(start, we1, True)

    tiles(vectors, tall, local)
    for d in order:
        sent.append(to_each(s1, b_all.at[y], sem_b, d))
    b_all[y] = piece(s1, y)[...]

    prepare(wf1, u_ref[0, 1, 0], -u_ref[0, 1, 1])

    def backward_map(i):
        rows = jnp.concatenate([u_ref[0, 0, 0, pl.ds(i, tall), :], -u_ref[0, 0, 1, pl.ds(i, tall), :]], axis=1)
        d_all[y, pl.ds(i, tall), :] = times(rows, wf1, False)

    tiles(width, tall, backward_map)
    sent += to_all(d_all, sem_d)
    prepare(wf0, u_ref[0, 0, 0], -u_ref[0, 0, 1])

    prepare(wc.at[y], c_all[y, :, :width], c_all[y, :, width:])
    for d in order:
        k = lax.rem(y + ysize - d, ysize)
        arrived(c_all.at[k], sem_c, d)
        prepare(wc.at[k], c_all[k, :, :width], c_all[k, :, width:])

    def group_forward(i):
        value = c_all[ysize - 1, pl.ds(i, tall), :]
        for k in reversed(range(ysize - 1)):
            value = times(value, wc.at[k], False)
        eo[pl.ds(i, tall), :] = value

    tiles(width, tall, group_forward)
    prepare(wp, eo[:width, :width], eo[:width, width:])
    for d in order:
        arrived(b_all.at[lax.rem(y + ysize - d, ysize)], sem_b, d)
    value = b_all[0]
    for k in range(1, ysize):
        value = times(value, wc.at[k], True) + b_all[k]
    qg[...] = value

    def group_backward():
        prepare(wd.at[y], d_all[y, :, :width], d_all[y, :, width:])
        for d in order:
            k = lax.rem(y + ysize - d, ysize)
            arrived(d_all.at[k], sem_d, d)
            prepare(wd.at[k], d_all[k, :, :width], d_all[k, :, width:])

        def compose(i):
            value = d_all[0, pl.ds(i, tall), :]
            for k in range(1, ysize):
                value = times(value, wd.at[k], False)
            win[pl.ds(i, tall), :] = value

        tiles(width, tall, compose)
        prepare(wq, win[:width, :width], win[:width, width:])

    late = z >= zsize // 2
    pl.when(late)(group_backward)

    @pl.when(z == 0)
    def _():
        vz[...] = jnp.zeros_like(vz)

    def hop(out, into, sems, s, device):
        return remote(out.at[pl.ds(s * sub, sub), :], into.at[pl.ds(s * sub, sub), :], sems, s, s, device)

    ahead, behind = {"z": lax.rem(z + 1, zsize)}, {"z": lax.rem(z + zsize - 1, zsize)}
    for s in range(SUBS):
        rows = pl.ds(s * sub, sub)

        @pl.when(z > 0)
        def _():
            hop(vz, vz, sem_fz, s, behind).wait_recv()

        @pl.when(z < zsize - 1)
        def _():
            vo[rows, :] = times(vz[rows, :], wp, True) + qg[rows, :]
            hop(vo, vz, sem_fz, s, ahead).start()

    def hand_out(k, value, staging, into, sems):
        staging[k] = value

        @pl.when(y == k)
        def _():
            piece(into, y)[...] = value

        @pl.when(y != k)
        def _():
            remote(staging.at[k], piece(into, y), sems, k, y, {"y": k}).start()

    def collect(into, sems, j):
        @pl.when(y != j)
        def _():
            remote(piece(into, j), piece(into, j), sems, j, j, {"y": j}).wait_recv()

    def handed_out(staging, into, sems):
        for k in range(ysize):
            @pl.when(y != k)
            def _():
                remote(staging.at[k], piece(into, y), sems, k, y, {"y": k}).wait_send()

    value = vz[...]
    for k in range(ysize):
        hand_out(k, value, vk, vin, sem_v)
        if k < ysize - 1:
            value = times(value, wc.at[k], True) + b_all[k]

    pl.when(jnp.logical_not(late))(group_backward)

    for j in range(ysize):
        collect(vin, sem_v, j)
        rows = pl.ds(j * chunk, chunk)
        value = vin[rows, :]
        first = s0[rows, :] - times(value, we0, True)
        second = s1[rows, :] + times(value, wc.at[y], True)
        y0[rows, :] = first
        y1[rows, :] = second
        ends = first - times(second, wf0, True)
        eo[rows, :] = ends

        @pl.when(y == j)
        def _():
            e_all[j] = ends

        @pl.when(y != j)
        def _():
            remote(eo.at[rows, :], e_all.at[y], sem_e, j, y, {"y": j}).start()

    for k in range(ysize):
        @pl.when(y != k)
        def _():
            remote(e_all.at[k], e_all.at[k], sem_e, k, k, {"y": k}).wait_recv()

    value = e_all[ysize - 1]
    for k in reversed(range(ysize - 1)):
        value = times(value, wd.at[k], True) + e_all[k]
    rg[...] = value

    @pl.when(z == zsize - 1)
    def _():
        wz[...] = jnp.zeros_like(wz)

    for s in range(SUBS):
        rows = pl.ds(s * sub, sub)

        @pl.when(z < zsize - 1)
        def _():
            hop(wz, wz, sem_bz, s, ahead).wait_recv()

        @pl.when(z > 0)
        def _():
            wo[rows, :] = times(wz[rows, :], wq, True) + rg[rows, :]
            hop(wo, wz, sem_bz, s, behind).start()

    value = wz[...]
    for k in reversed(range(ysize)):
        hand_out(k, value, wk, win, sem_w)
        if k > 0:
            value = times(value, wd.at[k], True) + e_all[k]

    wreal, wimag = w_ref[0, 0], w_ref[0, 1]
    for j in range(ysize):
        collect(win, sem_w, j)
        rows = pl.ds(j * chunk, chunk)
        second = y1[rows, :] - times(win[rows, :], wf1, True)
        first = y0[rows, :] - times(second, wf0, True)
        for n, part in enumerate((first, second)):
            real, imag = part[:, :width], part[:, width:]
            out_ref[n, rows, :width] = wreal * real - wimag * imag
            out_ref[n, rows, width:] = wreal * imag + wimag * real

    for copy in sent:
        copy.wait_send()
    handed_out(vk, vin, sem_v)
    handed_out(wk, win, sem_w)
    for j in range(ysize):
        @pl.when(y != j)
        def _():
            remote(eo.at[pl.ds(j * chunk, chunk), :], e_all.at[y], sem_e, j, y, {"y": j}).wait_send()
    for s in range(SUBS):
        @pl.when(z < zsize - 1)
        def _():
            hop(vo, vz, sem_fz, s, ahead).wait_send()

        @pl.when(z > 0)
        def _():
            hop(wo, wz, sem_bz, s, behind).wait_send()


def finish(
    dims, total_rows, x_ref, out_ref,
    other, cut, got, gram, g1, t1, g2, g3, h2, h1, wn, zs, turned, fin,
    sem_a, sem_x, sem_1, sem_2, sem_3, sem_4, sem_5, sem_6,
):
    xsize, zsize, ysize = dims
    x, core, z, y = (lax.axis_index(a) for a in AXES)
    poles = 2 * xsize
    pole = x * 2 + core
    vectors, width = x_ref.shape[1], x_ref.shape[2] // 2
    part = width // xsize
    own = vectors // poles
    line = own // ysize
    tall = min(128, vectors)

    def pole_of(d):
        p = lax.rem(pole + d, poles)
        return p, {"x": p // 2, "core": lax.rem(p, 2)}

    barrier = pltpu.get_barrier_semaphore()
    for d in range(1, poles):
        pl.semaphore_signal(barrier, inc=1, device_id=pole_of(d)[1], device_id_type=MESH_ID)
    for d in range(1, ysize):
        pl.semaphore_signal(barrier, inc=1, device_id={"y": lax.rem(y + d, ysize)}, device_id_type=MESH_ID)
    for d in range(1, zsize):
        pl.semaphore_signal(barrier, inc=1, device_id={"z": lax.rem(z + d, zsize)}, device_id_type=MESH_ID)
    pl.semaphore_wait(barrier, poles + ysize + zsize - 3)

    sent = []

    def go(src, dst, sems, d, device):
        copy = remote(src, dst, sems, d, d, device)
        copy.start()
        sent.append(copy)

    def land(dst, sems, d, device):
        remote(dst, dst, sems, d, d, device).wait_recv()

    def back(me, d, size):
        return lax.rem(me + size - d, size)

    sibling = {"core": 1 - core}
    go(x_ref.at[1 - core], other, sem_a, 0, sibling)
    land(other, sem_a, 0, sibling)
    pair = x_ref[core] + other[...]
    for j in range(xsize):
        cut[j] = jnp.concatenate(
            [pair[:, j * part : (j + 1) * part], pair[:, width + j * part : width + (j + 1) * part]], axis=1
        )
    for d in nearest_first(xsize):
        j = lax.rem(x + d, xsize)
        go(cut.at[j], got.at[x], sem_x, d, {"x": j})
    got[x] = cut[x]
    for d in nearest_first(xsize):
        j = back(x, d, xsize)
        land(got.at[j], sem_x, d, {"x": j})
    basis = got[0]
    for j in range(1, xsize):
        basis = basis + got[j]
    real, imag = basis[:, :part], basis[:, part:]
    lh, ll = halves(basis)
    rh, rl = halves(jnp.concatenate([real + imag, imag - real], axis=1))
    gram[...] = dot(lh, rh, True) + dot(ll, rh, True) + dot(lh, rl, True)

    def lines(ref, j, count):
        return ref.at[pl.ds(pl.multiple_of(j * count, count), count), :]

    for d in range(1, poles):
        p, device = pole_of(d)
        go(lines(gram, p, own), g1.at[pole], sem_1, d, device)
    g1[pole] = lines(gram, pole, own)[...]
    for d in range(1, poles):
        land(g1.at[back(pole, d, poles)], sem_1, d, pole_of(poles - d)[1])
    value = g1[0]
    for j in range(1, poles):
        value = value + g1[j]
    t1[...] = value
    for d in nearest_first(ysize):
        j = lax.rem(y + d, ysize)
        go(lines(t1, j, line), g2.at[y], sem_2, d, {"y": j})
    g2[y] = lines(t1, y, line)[...]
    for d in nearest_first(ysize):
        j = back(y, d, ysize)
        land(g2.at[j], sem_2, d, {"y": j})
    value = g2[0]
    for j in range(1, ysize):
        value = value + g2[j]
    g3[z] = value
    for d in nearest_first(zsize):
        go(g3.at[z], g3.at[z], sem_3, d, {"z": lax.rem(z + d, zsize)})
    for d in nearest_first(zsize):
        j = back(z, d, zsize)
        land(g3.at[j], sem_3, d, {"z": j})
    value = g3[0]
    for j in range(1, zsize):
        value = value + g3[j]
    lines(h2, y, line)[...] = value
    for d in nearest_first(ysize):
        go(lines(h2, y, line), lines(h2, y, line), sem_4, d, {"y": lax.rem(y + d, ysize)})
    for d in nearest_first(ysize):
        j = back(y, d, ysize)
        land(lines(h2, j, line), sem_4, d, {"y": j})
    lines(h1, pole, own)[...] = h2[...]
    for d in range(1, poles):
        go(h2, lines(h1, pole, own), sem_5, d, pole_of(d)[1])
    for d in range(1, poles):
        land(lines(h1, back(pole, d, poles), own), sem_5, d, pole_of(poles - d)[1])

    whole = h1[...]
    frob = jnp.sqrt(jnp.sum(whole * whole))
    flip = whole.T
    scale = -0.25 / frob
    eye = (
        lax.broadcasted_iota(jnp.int32, (vectors, vectors), 0)
        == lax.broadcasted_iota(jnp.int32, (vectors, vectors), 1)
    )
    first = jnp.where(eye, 1.5, 0.0) + scale * (whole + flip)
    minus = -scale * (whole - flip)
    prepare(wn.at[0], first, minus)
    zs[0, :, :vectors] = first
    zs[0, :, vectors:] = minus

    def square(i):
        rows = pl.ds(i, tall)
        zs[1, rows, :] = times(zs[0, rows, :], wn.at[0], False)

    tiles(vectors, tall, square)
    prepare(
        wn.at[1],
        zs[1, :, :vectors] - 1.5 * zs[0, :, :vectors],
        zs[1, :, vectors:] - 1.5 * zs[0, :, vectors:],
    )
    size = jnp.sqrt(total_rows / frob)
    stacked = jnp.concatenate(
        [basis, jnp.concatenate([-imag, real], axis=1)], axis=0
    )
    qh, ql = halves(stacked)
    turned[0] = qh
    turned[1] = ql

    def rotate(i):
        rows = pl.ds(i, tall)
        mix = 1.5 * zs[0, rows, :] + times(zs[1, rows, :], wn.at[1], False)
        gram_rows = times(mix, turned, False) * size
        cut[0, rows, :] = gram_rows

    for copy in sent:
        copy.wait_send()
    sent.clear()
    tiles(vectors, tall, rotate)
    for d in range(1, poles):
        p, device = pole_of(d)
        go(lines(cut.at[0], p, own), fin.at[pole], sem_6, d, device)
    fin[pole] = lines(cut.at[0], pole, own)[...]
    for d in range(1, poles):
        land(fin.at[back(pole, d, poles)], sem_6, d, pole_of(poles - d)[1])
    slots = [2 * j + n for n in range(2) for j in range(xsize)]
    out_ref[0] = jnp.concatenate([fin[k][:, :part] for k in slots], axis=1)
    out_ref[1] = jnp.concatenate([fin[k][:, part:] for k in slots], axis=1)
    for copy in sent:
        copy.wait_send()


def vmem():
    return pl.BlockSpec(memory_space=pltpu.VMEM)


def shards(sizes, subspace, pivots, lower_blocks, upper_blocks, pole_weights):
    xsize, zsize, ysize = sizes
    vectors, width = subspace.shape[1], pivots.shape[-1]
    wide = 2 * width
    chunk = vectors // ysize
    weight = (2, wide, wide)

    def dma(count):
        return pltpu.SemaphoreType.DMA((2, count))

    solved = pl.pallas_call(
        functools.partial(sweeps, (ysize, zsize)),
        out_shape=jax.ShapeDtypeStruct((2, vectors, wide), F32),
        in_specs=[vmem()] * 4 + [pl.BlockSpec(memory_space=pltpu.SMEM)],
        out_specs=vmem(),
        scratch_shapes=[pltpu.VMEM(weight, BF16)] * 4
        + [pltpu.VMEM((2, *weight), BF16)]
        + [pltpu.VMEM((ysize, *weight), BF16)] * 2
        + [pltpu.VMEM(weight, BF16)] * 2
        + [pltpu.VMEM((ysize, width, wide), F32)] * 2
        + [pltpu.VMEM((ysize, chunk, wide), F32)] * 2
        + [pltpu.VMEM((chunk, wide), F32)] * 2
        + [pltpu.VMEM((vectors, wide), F32)] * 7
        + [pltpu.VMEM((chunk, wide), F32)] * 4
        + [pltpu.VMEM((ysize, chunk, wide), F32)] * 2
        + [dma(ysize)] * 6
        + [dma(SUBS)] * 2,
        compiler_params=pltpu.CompilerParams(
            collective_id=0, has_side_effects=True, vmem_limit_bytes=56 * 2**20
        ),
        name="sweeps",
    )(subspace, pivots, lower_blocks, upper_blocks, pole_weights)

    poles = 2 * xsize
    part = width // xsize
    own = vectors // poles
    line = own // ysize
    total_rows = float(2 * width * ysize * zsize)
    return pl.pallas_call(
        functools.partial(finish, (xsize, zsize, ysize), total_rows),
        out_shape=jax.ShapeDtypeStruct((2, own, wide), F32),
        in_specs=[vmem()],
        out_specs=vmem(),
        scratch_shapes=[
            pltpu.VMEM((vectors, wide), F32),
            pltpu.VMEM((xsize, vectors, 2 * part), F32),
            pltpu.VMEM((xsize, vectors, 2 * part), F32),
            pltpu.VMEM((vectors, vectors), F32),
            pltpu.VMEM((poles, own, vectors), F32),
            pltpu.VMEM((own, vectors), F32),
            pltpu.VMEM((ysize, line, vectors), F32),
            pltpu.VMEM((zsize, line, vectors), F32),
            pltpu.VMEM((own, vectors), F32),
            pltpu.VMEM((vectors, vectors), F32),
            pltpu.VMEM((2, 2, 2 * vectors, 2 * vectors), BF16),
            pltpu.VMEM((2, vectors, 2 * vectors), F32),
            pltpu.VMEM((2, 2 * vectors, 2 * part), BF16),
            pltpu.VMEM((poles, own, 2 * part), F32),
            dma(1),
            dma(xsize),
            dma(poles),
            dma(ysize),
            dma(zsize),
            dma(ysize),
            dma(poles),
            dma(poles),
        ],
        compiler_params=pltpu.CompilerParams(
            collective_id=1, has_side_effects=True, vmem_limit_bytes=56 * 2**20
        ),
        name="finish",
    )(solved)


def build(mesh, sizes):
    xsize, zsize, ysize = sizes
    torus = Mesh(mesh.devices.reshape(xsize, 2, zsize, ysize), AXES)
    pole, rows = ("x", "core"), ("z", "y")
    return jax.shard_map(
        functools.partial(shards, sizes),
        mesh=torus,
        in_specs=(
            P(None, None, rows),
            P(pole, rows, None, None, None),
            P(pole, rows, None, None, None),
            P(pole, rows, None, None, None),
            P(pole, None),
        ),
        out_specs=P(None, pole, rows),
        check_vma=False,
    )


def solution(mesh):
    return build(mesh, (mesh.shape["pole"] // 2, mesh.shape["rows"] // 4, 4))
```

time: 678 us -> 177 us (0.26)
  the two profiles are of different devices: /device:TPU:2 before, /device:TPU:1 now
where the time goes in v1:
time: 177 us
  Pallas kernels  176 us (99%)
    pallas_call x1, Pallas kernels, shards(): pl.pallas_call(functools.partial(sweeps, (ysize, zsize)), out_shape=jax.S...  116 us
    pallas_call x1, Pallas kernels, shards(): pl.pallas_call(functools.partial(finish, (xsize, zsize, ysize), total_row...  59.4 us

profile of v1, /device:TPU:1, one launch (start us, length us, event | category | flops | bytes accessed | tf_op | source)
XLA Modules:
  0.0 177.3 jit_solution(16600404184477121866)
XLA Ops:
  0.0 116.3 %sweeps.1.x_ref = f32[2,256,512]{2,1,0:T(8,128)} custom-call(f32[2,256,512]{2,1,0:T(8,128)} %f_ref.1, f32[1,2,2,256,256]{4,3,2,1,0:T(8,128)} %g_ref.1, f32[1,2,2,256,256]{4,3,2,1,0:T(8,128)} %e_ref.1, f32[1,2,2,256,256]{4,3,2,1,0:T(8,128)} %u_ref.1, f32[1,2]{1,0:T(1,128)} %w_ref.1), custom_call_target="tpu_custom_call" | custom-call | tf_op jit(solution)/shard_map/sweeps/pallas_call | solution.py:498
  116.3 59.4 %finish.1 = f32[2,32,512]{2,1,0:T(8,128)} custom-call(f32[2,256,512]{2,1,0:T(8,128)} %sweeps.1.x_ref), custom_call_target="tpu_custom_call" | custom-call | tf_op jit(solution)/shard_map/finish/pallas_call | solution.py:526
  175.7 1.6 copy.7

commit v2 on v1

v2 whole, which is shorter than its diff:
```python
import functools

import jax
import jax.numpy as jnp
from jax import lax
from jax.experimental import pallas as pl
from jax.experimental.pallas import tpu as pltpu
from jax.sharding import Mesh
from jax.sharding import PartitionSpec as P

F32 = jnp.float32
BF16 = jnp.bfloat16
MESH_ID = pl.DeviceIdType.MESH
AXES = ("x", "core", "z", "y")
SUBS = 4


def halves(value):
    high = value.astype(BF16)
    return high, (value - high.astype(F32)).astype(BF16)


def dot(left, right, trans):
    dims = (((1,), (1 if trans else 0,)), ((), ()))
    return lax.dot_general(left, right, dims, preferred_element_type=F32)


def times(rows, weights, trans):
    high, low = halves(rows)
    count = rows.shape[0]
    both = dot(jnp.concatenate([high, low], axis=0), weights[0], trans)
    return both[:count] + both[count:] + dot(high, weights[1], trans)


def prepare(weights, real, minus):
    size = real.shape[0]
    for part, (r, m) in enumerate(zip(halves(real), halves(minus))):
        weights[part, :size, :size] = r
        weights[part, :size, size:] = m
        weights[part, size:, :size] = -m
        weights[part, size:, size:] = r


def tiles(count, size, body):
    if count == size:
        body(0)
        return

    def step(i, carry):
        body(pl.multiple_of(i * size, size))
        return carry

    lax.fori_loop(0, count // size, step, 0)


def remote(src, dst, sems, slot_out, slot_in, device):
    return pltpu.make_async_remote_copy(
        src_ref=src,
        dst_ref=dst,
        send_sem=sems.at[0, slot_out],
        recv_sem=sems.at[1, slot_in],
        device_id=device,
        device_id_type=MESH_ID,
    )


def nearest_first(count):
    return sorted(range(1, count), key=lambda d: min(d, count - d))


def step_kernel(
    dims, total_rows, f_hbm, g_hbm, e_hbm, u_hbm, w_ref, out_ref,
    f_ref, g_ref, e_ref, u_ref,
    we0, we1, wf0, wf1, wg, wc, wd, wp, wq, wh,
    c_all, d_all, b_all, e_all, qg, rg, s0, s1, y0, y1, e0, eo, vin, win, tmp,
    vz, vo, wz, wo, vk, wk,
    xs, other, cut, got, gram, g1, t1, g2, g3, h2, h1, wn, zs, turned, spun, fin,
    sem_in, sem_c, sem_b, sem_d, sem_v, sem_e, sem_w, sem_fz, sem_bz,
    sem_a, sem_x, sem_1, sem_2, sem_3, sem_4, sem_5, sem_6,
):
    xsize, zsize, ysize = dims
    x, core, z, y = (lax.axis_index(a) for a in AXES)
    poles = 2 * xsize
    pole = x * 2 + core
    vectors, width = f_ref.shape[1], g_ref.shape[-1]
    chunk = vectors // ysize
    sub = chunk // SUBS
    tall = min(128, width)
    part = width // xsize
    own = vectors // poles
    line = own // ysize
    order = nearest_first(ysize)

    def pole_of(d):
        p = lax.rem(pole + d, poles)
        return p, {"x": p // 2, "core": lax.rem(p, 2)}

    def along(axis, me, d, size):
        return {axis: lax.rem(me + d, size)}

    barrier = pltpu.get_barrier_semaphore()
    for d in range(1, ysize):
        pl.semaphore_signal(barrier, inc=1, device_id=along("y", y, d, ysize), device_id_type=MESH_ID)
    for d in range(1, zsize):
        pl.semaphore_signal(barrier, inc=1, device_id=along("z", z, d, zsize), device_id_type=MESH_ID)
    for d in range(1, poles):
        pl.semaphore_signal(barrier, inc=1, device_id=pole_of(d)[1], device_id_type=MESH_ID)

    loads = [
        pltpu.make_async_copy(a, b, sem_in.at[i])
        for i, (a, b) in enumerate(((e_hbm, e_ref), (u_hbm, u_ref), (g_hbm, g_ref), (f_hbm, f_ref)))
    ]
    for load in loads:
        load.start()

    sent = []

    def go(src, dst, sems, d, device):
        copy = remote(src, dst, sems, d, d, device)
        copy.start()
        sent.append(copy)

    def land(dst, sems, d, device):
        remote(dst, dst, sems, d, d, device).wait_recv()

    def back(me, d, size):
        return lax.rem(me + size - d, size)

    def lines(ref, j, count):
        return ref.at[pl.ds(pl.multiple_of(j * count, count), count), :]

    def piece(ref, j):
        return lines(ref, j, chunk)

    loads[0].wait()
    prepare(we0, e_ref[0, 0, 0], -e_ref[0, 0, 1])

    def forward_map(i):
        rows = jnp.concatenate([e_ref[0, 1, 0, pl.ds(i, tall), :], -e_ref[0, 1, 1, pl.ds(i, tall), :]], axis=1)
        c_all[y, pl.ds(i, tall), :] = times(rows, we0, False)

    tiles(width, tall, forward_map)
    pl.semaphore_wait(barrier, ysize + zsize + poles - 3)

    half = width // 2
    right, left = along("y", y, 1, ysize), along("y", y, ysize - 1, ysize)
    after, ahead_y = back(y, 1, ysize), lax.rem(y + 1, ysize)

    def half_of(k, h):
        return c_all.at[k, pl.ds(h * half, half), :]

    go(half_of(y, 0), half_of(y, 0), sem_c, 0, right)
    if ysize > 2:
        go(half_of(y, 1), half_of(y, 1), sem_c, 2, left)
    go(half_of(y, 1), half_of(y, 1), sem_c, 1, right)
    if ysize > 2:
        go(half_of(y, 0), half_of(y, 0), sem_c, 3, left)

    loads[2].wait()
    prepare(wg.at[0], g_ref[0, 0, 0], -g_ref[0, 0, 1])
    prepare(wg.at[1], g_ref[0, 1, 0], -g_ref[0, 1, 1])
    prepare(we1, e_ref[0, 1, 0], -e_ref[0, 1, 1])
    loads[3].wait()

    def local(i):
        rows = pl.ds(i, tall)
        first = jnp.concatenate([f_ref[0, rows, :width], f_ref[1, rows, :width]], axis=1)
        second = jnp.concatenate([f_ref[0, rows, width:], f_ref[1, rows, width:]], axis=1)
        start = times(first, wg.at[0], True)
        s0[rows, :] = start
        s1[rows, :] = times(second, wg.at[1], True) - times(start, we1, True)

    tiles(vectors, tall, local)
    for d in order:
        go(piece(s1, lax.rem(y + d, ysize)), b_all.at[y], sem_b, d, along("y", y, d, ysize))
    b_all[y] = piece(s1, y)[...]

    def pass_on():
        land(half_of(after, 0), sem_c, 0, left)
        if ysize > 2:
            go(half_of(after, 0), half_of(after, 0), sem_c, 4, right)
            land(half_of(ahead_y, 1), sem_c, 2, right)
            go(half_of(ahead_y, 1), half_of(ahead_y, 1), sem_c, 5, left)

    loads[1].wait()
    prepare(wf1, u_ref[0, 1, 0], -u_ref[0, 1, 1])
    prepare(wf0, u_ref[0, 0, 0], -u_ref[0, 0, 1])
    prepare(wc.at[y], c_all[y, :, :width], c_all[y, :, width:])

    def backward_map(i):
        rows = pl.ds(i, tall)
        upper = jnp.concatenate([u_ref[0, 0, 0, rows, :], -u_ref[0, 0, 1, rows, :]], axis=1)
        d_all[y, rows, :] = times(upper, wf1, False)
        lower = jnp.concatenate([e_ref[0, 0, 0, rows, :], -e_ref[0, 0, 1, rows, :]], axis=1)
        tmp[rows, :] = -lower - times(upper, wc.at[y], False)

    tiles(width, tall, backward_map)
    pass_on()
    prepare(wh, tmp[:width, :width], tmp[:width, width:])

    def local_ends(i):
        rows = pl.ds(i, tall)
        e0[rows, :] = s0[rows, :] - times(s1[rows, :], wf0, True)

    tiles(vectors, tall, local_ends)

    land(half_of(after, 1), sem_c, 1, left)
    prepare(wc.at[after], c_all[after, :, :width], c_all[after, :, width:])
    if ysize > 2:
        land(half_of(ahead_y, 0), sem_c, 3, right)
        prepare(wc.at[ahead_y], c_all[ahead_y, :, :width], c_all[ahead_y, :, width:])
        far = lax.rem(y + 2, ysize)
        land(half_of(far, 0), sem_c, 4, left)
        land(half_of(far, 1), sem_c, 5, right)
        prepare(wc.at[far], c_all[far, :, :width], c_all[far, :, width:])
    for d in order:
        land(b_all.at[back(y, d, ysize)], sem_b, d, along("y", y, ysize - d, ysize))
    for d in order:
        go(d_all.at[y], d_all.at[y], sem_d, d, along("y", y, d, ysize))

    value = b_all[0]
    for k in range(1, ysize):
        value = times(value, wc.at[k], True) + b_all[k]
    qg[...] = value

    def hop(out, into, sems, s, device):
        return remote(out.at[pl.ds(s * sub, sub), :], into.at[pl.ds(s * sub, sub), :], sems, s, s, device)

    ahead, behind = along("z", z, 1, zsize), along("z", z, zsize - 1, zsize)

    @pl.when(z == 0)
    def _():
        for s in range(SUBS):
            hop(qg, vz, sem_fz, s, ahead).start()
        vz[...] = jnp.zeros_like(vz)

    @pl.when(jnp.logical_and(z > 0, z < zsize - 1))
    def _():
        def group_forward(i):
            value = c_all[ysize - 1, pl.ds(i, tall), :]
            for k in reversed(range(ysize - 1)):
                value = times(value, wc.at[k], False)
            tmp[pl.ds(i, tall), :] = value

        tiles(width, tall, group_forward)
        prepare(wp, tmp[:width, :width], tmp[:width, width:])

    for s in range(SUBS):
        rows = pl.ds(s * sub, sub)

        @pl.when(z > 0)
        def _():
            hop(vz, vz, sem_fz, s, behind).wait_recv()

        @pl.when(jnp.logical_and(z > 0, z < zsize - 1))
        def _():
            vo[rows, :] = times(vz[rows, :], wp, True) + qg[rows, :]
            hop(vo, vz, sem_fz, s, ahead).start()

    def hand_out(k, value, staging, into, sems):
        staging[k] = value

        @pl.when(y == k)
        def _():
            piece(into, y)[...] = value

        @pl.when(y != k)
        def _():
            remote(staging.at[k], piece(into, y), sems, k, y, {"y": k}).start()

    def handed_out(staging, into, sems):
        for k in range(ysize):
            @pl.when(y != k)
            def _():
                remote(staging.at[k], piece(into, y), sems, k, y, {"y": k}).wait_send()

    value = vz[...]
    for k in range(ysize):
        hand_out(k, value, vk, vin, sem_v)
        if k < ysize - 1:
            value = times(value, wc.at[k], True) + b_all[k]

    prepare(wd.at[y], d_all[y, :, :width], d_all[y, :, width:])
    for d in order:
        k = back(y, d, ysize)
        land(d_all.at[k], sem_d, d, along("y", y, ysize - d, ysize))
        prepare(wd.at[k], d_all[k, :, :width], d_all[k, :, width:])

    for d in [0] + order:
        j = lax.rem(y + d, ysize)
        rows = pl.ds(pl.multiple_of(j * chunk, chunk), chunk)
        if d:
            remote(vin.at[rows, :], vin.at[rows, :], sem_v, j, j, {"y": j}).wait_recv()
        ends = e0[rows, :] + times(vin[rows, :], wh, True)
        if d:
            eo[rows, :] = ends
            remote(eo.at[rows, :], e_all.at[y], sem_e, j, y, {"y": j}).start()
        else:
            e_all[y] = ends

    def swept(i):
        rows = pl.ds(i, tall)
        value = vin[rows, :]
        y0[rows, :] = s0[rows, :] - times(value, we0, True)
        y1[rows, :] = s1[rows, :] + times(value, wc.at[y], True)

    tiles(vectors, tall, swept)

    @pl.when(jnp.logical_and(z > 0, z < zsize - 1))
    def _():
        def compose(i):
            value = d_all[0, pl.ds(i, tall), :]
            for k in range(1, ysize):
                value = times(value, wd.at[k], False)
            tmp[pl.ds(i, tall), :] = value

        tiles(width, tall, compose)
        prepare(wq, tmp[:width, :width], tmp[:width, width:])

    for d in order:
        j = lax.rem(y + d, ysize)
        remote(e_all.at[j], e_all.at[j], sem_e, j, j, {"y": j}).wait_recv()
    value = e_all[ysize - 1]
    for k in reversed(range(ysize - 1)):
        value = times(value, wd.at[k], True) + e_all[k]
    rg[...] = value

    @pl.when(z == zsize - 1)
    def _():
        for s in range(SUBS):
            hop(rg, wz, sem_bz, s, behind).start()
        wz[...] = jnp.zeros_like(wz)

    for s in range(SUBS):
        rows = pl.ds(s * sub, sub)

        @pl.when(z < zsize - 1)
        def _():
            hop(wz, wz, sem_bz, s, ahead).wait_recv()

        @pl.when(jnp.logical_and(z > 0, z < zsize - 1))
        def _():
            wo[rows, :] = times(wz[rows, :], wq, True) + rg[rows, :]
            hop(wo, wz, sem_bz, s, behind).start()

    value = wz[...]
    for k in reversed(range(ysize)):
        hand_out(k, value, wk, win, sem_w)
        if k > 0:
            value = times(value, wd.at[k], True) + e_all[k]

    sibling = {"core": 1 - core}
    wreal, wimag = w_ref[0, 0], w_ref[0, 1]

    def rows_of(d):
        j = lax.rem(y + d, ysize)
        return j, pl.ds(pl.multiple_of(j * chunk, chunk), chunk)

    def over_x(turn, d):
        _, rows = rows_of(d)
        land(other.at[rows, :], sem_a, turn, sibling)
        pair = xs[core, rows, :] + other[rows, :]
        for j in range(xsize):
            cut[j, rows, :] = jnp.concatenate(
                [pair[:, j * part : (j + 1) * part], pair[:, width + j * part : width + (j + 1) * part]], axis=1
            )
        for step in nearest_first(xsize):
            go(
                cut.at[lax.rem(x + step, xsize), rows, :],
                got.at[x, rows, :],
                sem_x,
                turn * xsize + step,
                along("x", x, step, xsize),
            )
        got[x, rows, :] = cut[x, rows, :]

    turns = [0] + order
    for turn, d in enumerate(turns):
        j, rows = rows_of(d)
        if d:
            remote(win.at[rows, :], win.at[rows, :], sem_w, j, j, {"y": j}).wait_recv()
        second = y1[rows, :] - times(win[rows, :], wf1, True)
        first = y0[rows, :] - times(second, wf0, True)
        for n, solved in enumerate((first, second)):
            real, imag = solved[:, :width], solved[:, width:]
            xs[n, rows, :width] = wreal * real - wimag * imag
            xs[n, rows, width:] = wreal * imag + wimag * real
        go(xs.at[1 - core, rows, :], other.at[rows, :], sem_a, turn, sibling)
        if turn:
            over_x(turn - 1, turns[turn - 1])
    over_x(len(turns) - 1, turns[-1])
    for turn, d in enumerate(turns):
        _, rows = rows_of(d)
        for step in nearest_first(xsize):
            j = back(x, step, xsize)
            land(got.at[j, rows, :], sem_x, turn * xsize + step, {"x": j})
    basis = got[0]
    for j in range(1, xsize):
        basis = basis + got[j]
    real, imag = basis[:, :part], basis[:, part:]
    lh, ll = halves(basis)
    rh, rl = halves(jnp.concatenate([real + imag, imag - real], axis=1))
    gram[...] = dot(lh, rh, True) + dot(ll, rh, True) + dot(lh, rl, True)

    for d in range(1, poles):
        p, device = pole_of(d)
        go(lines(gram, p, own), g1.at[pole], sem_1, d, device)
    g1[pole] = lines(gram, pole, own)[...]
    for d in range(1, poles):
        land(g1.at[back(pole, d, poles)], sem_1, d, pole_of(poles - d)[1])
    value = g1[0]
    for j in range(1, poles):
        value = value + g1[j]
    t1[...] = value
    for d in nearest_first(ysize):
        j = lax.rem(y + d, ysize)
        go(lines(t1, j, line), g2.at[y], sem_2, d, {"y": j})
    g2[y] = lines(t1, y, line)[...]
    for d in nearest_first(ysize):
        j = back(y, d, ysize)
        land(g2.at[j], sem_2, d, {"y": j})
    value = g2[0]
    for j in range(1, ysize):
        value = value + g2[j]
    g3[z] = value
    for d in nearest_first(zsize):
        go(g3.at[z], g3.at[z], sem_3, d, {"z": lax.rem(z + d, zsize)})
    for d in nearest_first(zsize):
        j = back(z, d, zsize)
        land(g3.at[j], sem_3, d, {"z": j})
    value = g3[0]
    for j in range(1, zsize):
        value = value + g3[j]
    lines(h2, y, line)[...] = value
    for d in nearest_first(ysize):
        go(lines(h2, y, line), lines(h2, y, line), sem_4, d, {"y": lax.rem(y + d, ysize)})
    for d in nearest_first(ysize):
        j = back(y, d, ysize)
        land(lines(h2, j, line), sem_4, d, {"y": j})
    lines(h1, pole, own)[...] = h2[...]
    for d in range(1, poles):
        go(h2, lines(h1, pole, own), sem_5, d, pole_of(d)[1])
    for d in range(1, poles):
        land(lines(h1, back(pole, d, poles), own), sem_5, d, pole_of(poles - d)[1])

    whole = h1[...]
    frob = jnp.sqrt(jnp.sum(whole * whole))
    flip = whole.T
    scale = -0.25 / frob
    eye = (
        lax.broadcasted_iota(jnp.int32, (vectors, vectors), 0)
        == lax.broadcasted_iota(jnp.int32, (vectors, vectors), 1)
    )
    first = jnp.where(eye, 1.5, 0.0) + scale * (whole + flip)
    minus = -scale * (whole - flip)
    prepare(wn.at[0], first, minus)
    zs[0, :, :vectors] = first
    zs[0, :, vectors:] = minus

    def square(i):
        rows = pl.ds(i, tall)
        zs[1, rows, :] = times(zs[0, rows, :], wn.at[0], False)

    tiles(vectors, tall, square)
    prepare(
        wn.at[1],
        zs[1, :, :vectors] - 1.5 * zs[0, :, :vectors],
        zs[1, :, vectors:] - 1.5 * zs[0, :, vectors:],
    )
    size = jnp.sqrt(total_rows / frob)
    stacked = jnp.concatenate(
        [basis, jnp.concatenate([-imag, real], axis=1)], axis=0
    )
    qh, ql = halves(stacked)
    turned[0] = qh
    turned[1] = ql

    def rotate(i):
        rows = pl.ds(i, tall)
        mix = 1.5 * zs[0, rows, :] + times(zs[1, rows, :], wn.at[1], False)
        spun[rows, :] = times(mix, turned, False) * size

    tiles(vectors, tall, rotate)
    for d in range(1, poles):
        p, device = pole_of(d)
        go(lines(spun, p, own), fin.at[pole], sem_6, d, device)
    fin[pole] = lines(spun, pole, own)[...]
    for d in range(1, poles):
        land(fin.at[back(pole, d, poles)], sem_6, d, pole_of(poles - d)[1])
    slots = [2 * j + n for n in range(2) for j in range(xsize)]
    out_ref[0] = jnp.concatenate([fin[k][:, :part] for k in slots], axis=1)
    out_ref[1] = jnp.concatenate([fin[k][:, part:] for k in slots], axis=1)
    for copy in sent:
        copy.wait_send()
    handed_out(vk, vin, sem_v)
    handed_out(wk, win, sem_w)
    for d in order:
        j, rows = rows_of(d)
        remote(eo.at[rows, :], e_all.at[y], sem_e, j, y, {"y": j}).wait_send()
    for s in range(SUBS):
        @pl.when(z < zsize - 1)
        def _():
            hop(vo, vz, sem_fz, s, ahead).wait_send()

        @pl.when(z > 0)
        def _():
            hop(wo, wz, sem_bz, s, behind).wait_send()


def shards(sizes, subspace, pivots, lower_blocks, upper_blocks, pole_weights):
    xsize, zsize, ysize = sizes
    vectors, width = subspace.shape[1], pivots.shape[-1]
    wide = 2 * width
    chunk = vectors // ysize
    poles = 2 * xsize
    part = width // xsize
    own = vectors // poles
    line = own // ysize
    total_rows = float(2 * width * ysize * zsize)

    def dma(count):
        return pltpu.SemaphoreType.DMA((2, count))

    def f32(*shape):
        return pltpu.VMEM(shape, F32)

    def prepared(*counts):
        return pltpu.VMEM((*counts, 2, wide, wide), BF16)

    anywhere = pl.BlockSpec(memory_space=pl.ANY)
    return pl.pallas_call(
        functools.partial(step_kernel, (xsize, zsize, ysize), total_rows),
        out_shape=jax.ShapeDtypeStruct((2, own, wide), F32),
        in_specs=[anywhere] * 4 + [pl.BlockSpec(memory_space=pltpu.SMEM)],
        out_specs=pl.BlockSpec(memory_space=pltpu.VMEM),
        scratch_shapes=[f32(*a.shape) for a in (subspace, pivots, lower_blocks, upper_blocks)]
        + [prepared()] * 4
        + [prepared(2)]
        + [prepared(ysize)] * 2
        + [prepared()] * 3
        + [f32(ysize, width, wide)] * 2
        + [f32(ysize, chunk, wide)] * 2
        + [f32(chunk, wide)] * 2
        + [f32(vectors, wide)] * 9
        + [f32(chunk, wide)] * 4
        + [f32(ysize, chunk, wide)] * 2
        + [
            f32(2, vectors, wide),
            f32(vectors, wide),
            f32(xsize, vectors, 2 * part),
            f32(xsize, vectors, 2 * part),
            f32(vectors, vectors),
            f32(poles, own, vectors),
            f32(own, vectors),
            f32(ysize, line, vectors),
            f32(zsize, line, vectors),
            f32(own, vectors),
            f32(vectors, vectors),
            pltpu.VMEM((2, 2, 2 * vectors, 2 * vectors), BF16),
            f32(2, vectors, 2 * vectors),
            pltpu.VMEM((2, 2 * vectors, 2 * part), BF16),
            f32(vectors, 2 * part),
            f32(poles, own, 2 * part),
            pltpu.SemaphoreType.DMA((4,)),
            dma(6),
        ]
        + [dma(ysize)] * 5
        + [dma(SUBS)] * 2
        + [
            dma(ysize),
            dma(ysize * xsize),
            dma(poles),
            dma(ysize),
            dma(zsize),
            dma(ysize),
            dma(poles),
            dma(poles),
        ],
        compiler_params=pltpu.CompilerParams(
            collective_id=0, has_side_effects=True, vmem_limit_bytes=60 * 2**20
        ),
        name="step",
    )(subspace, pivots, lower_blocks, upper_blocks, pole_weights)


def build(mesh, sizes):
    xsize, zsize, ysize = sizes
    torus = Mesh(mesh.devices.reshape(xsize, 2, zsize, ysize), AXES)
    pole, rows = ("x", "core"), ("z", "y")
    return jax.shard_map(
        functools.partial(shards, sizes),
        mesh=torus,
        in_specs=(
            P(None, None, rows),
            P(pole, rows, None, None, None),
            P(pole, rows, None, None, None),
            P(pole, rows, None, None, None),
            P(pole, None),
        ),
        out_specs=P(None, pole, rows),
        check_vma=False,
    )


def solution(mesh):
    return build(mesh, (mesh.shape["pole"] // 2, mesh.shape["rows"] // 4, 4))
```

time: 177 us -> 149 us (0.84)
  Pallas kernels: 176 us -> 147 us
    pallas_call x2 -> x1, Pallas kernels: 176 us -> 147 us  [shards(): pl.pallas_call(functools.partial(step_kernel, (xsize, zsize, ysize), tota...]
where the time goes in v2:
time: 149 us; the launch traced here: 148 us
  Pallas kernels  147 us (99%)
  local copies, waits for them, and re-layouts  1.57 us (1%)
    pallas_call x1, Pallas kernels, shards(): pl.pallas_call(functools.partial(step_kernel, (xsize, zsize, ysize), tota...  147 us

profile of v2, /device:TPU:1, one launch (start us, length us, event | category | flops | bytes accessed | tf_op | source)
XLA Modules:
  0.0 148.3 jit_solution(3323665560029211901)
XLA Ops:
  0.0 146.7 %step.1 = f32[2,32,512]{2,1,0:T(8,128)} custom-call(f32[2,256,512]{2,1,0:T(8,128)} %f_hbm.1, f32[1,2,2,256,256]{4,3,2,1,0:T(8,128)} %g_hbm.1, f32[1,2,2,256,256]{4,3,2,1,0:T(8,128)} %e_hbm.1, f32[1,2,2,256,256]{4,3,2,1,0:T(8,128)} %u_hbm.1, f32[1,2]{1,0:T(1,128)} %w_ref.1), custom_call_target="tpu_custom_call" | custom-call | tf_op jit(solution)/shard_map/step/pallas_call | solution.py:531
  146.7 1.6 %copy.7 = f32[2,32,512]{2,1,0:T(8,128)} copy(f32[2,32,512]{2,1,0:T(8,128)} %step.1) | data formatting | bytes 262144

commit v3 on v2

--- a/solution.py
+++ b/solution.py
@@ -71,11 +71,11 @@
 def step_kernel(
     dims, total_rows, f_hbm, g_hbm, e_hbm, u_hbm, w_ref, out_ref,
     f_ref, g_ref, e_ref, u_ref,
-    we0, we1, wf0, wf1, wg, wc, wd, wp, wq, wh,
-    c_all, d_all, b_all, e_all, qg, rg, s0, s1, y0, y1, e0, eo, vin, win, tmp,
+    we0, we1, wf0, wf1, wg, wc, wd, wp, wq, wh, wj, wz1, wa0, wa1,
+    c_all, d_all, b_all, e_all, qg, rg, rj, rz, s0, s1, y0, y1, e0, eo, vin, win, tmp, wb, dg, dz, am,
     vz, vo, wz, wo, vk, wk,
     xs, other, cut, got, gram, g1, t1, g2, g3, h2, h1, wn, zs, turned, spun, fin,
-    sem_in, sem_c, sem_b, sem_d, sem_v, sem_e, sem_w, sem_fz, sem_bz,
+    sem_in, sem_c, sem_b, sem_d, sem_v, sem_e, sem_r, sem_w, sem_fz, sem_bz, sem_one, sem_far,
     sem_a, sem_x, sem_1, sem_2, sem_3, sem_4, sem_5, sem_6,
 ):
     xsize, zsize, ysize = dims
@@ -144,17 +144,39 @@
 
     half = width // 2
     right, left = along("y", y, 1, ysize), along("y", y, ysize - 1, ysize)
-    after, ahead_y = back(y, 1, ysize), lax.rem(y + 1, ysize)
-
-    def half_of(k, h):
-        return c_all.at[k, pl.ds(h * half, half), :]
-
-    go(half_of(y, 0), half_of(y, 0), sem_c, 0, right)
-    if ysize > 2:
-        go(half_of(y, 1), half_of(y, 1), sem_c, 2, left)
-    go(half_of(y, 1), half_of(y, 1), sem_c, 1, right)
-    if ysize > 2:
-        go(half_of(y, 0), half_of(y, 0), sem_c, 3, left)
+    before, beyond, far = back(y, 1, ysize), lax.rem(y + 1, ysize), lax.rem(y + 2, ysize)
+
+    def half_of(store, k, h):
+        return store.at[k, pl.ds(h * half, half), :]
+
+    def share(store, sems):
+        for slot, h, device in ((0, 0, right), (2, 1, left), (1, 1, right), (3, 0, left)):
+            if ysize > 2 or slot < 2:
+                go(half_of(store, y, h), half_of(store, y, h), sems, slot, device)
+
+    def onward(store, sems):
+        first, second = half_of(store, before, 0), half_of(store, beyond, 1)
+        return remote(first, first, sems, 4, 4, right), remote(second, second, sems, 5, 5, left)
+
+    def pass_on(store, sems):
+        land(half_of(store, before, 0), sems, 0, left)
+        if ysize > 2:
+            to_right, to_left = onward(store, sems)
+            to_right.start()
+            land(half_of(store, beyond, 1), sems, 2, right)
+            to_left.start()
+
+    def take(store, sems, weights):
+        land(half_of(store, before, 1), sems, 1, left)
+        prepare(weights.at[before], store[before, :, :width], store[before, :, width:])
+        if ysize > 2:
+            land(half_of(store, beyond, 0), sems, 3, right)
+            prepare(weights.at[beyond], store[beyond, :, :width], store[beyond, :, width:])
+            land(half_of(store, far, 0), sems, 4, left)
+            land(half_of(store, far, 1), sems, 5, right)
+            prepare(weights.at[far], store[far, :, :width], store[far, :, width:])
+
+    share(c_all, sem_c)
 
     loads[2].wait()
     prepare(wg.at[0], g_ref[0, 0, 0], -g_ref[0, 0, 1])
@@ -175,13 +197,6 @@
         go(piece(s1, lax.rem(y + d, ysize)), b_all.at[y], sem_b, d, along("y", y, d, ysize))
     b_all[y] = piece(s1, y)[...]
 
-    def pass_on():
-        land(half_of(after, 0), sem_c, 0, left)
-        if ysize > 2:
-            go(half_of(after, 0), half_of(after, 0), sem_c, 4, right)
-            land(half_of(ahead_y, 1), sem_c, 2, right)
-            go(half_of(ahead_y, 1), half_of(ahead_y, 1), sem_c, 5, left)
-
     loads[1].wait()
     prepare(wf1, u_ref[0, 1, 0], -u_ref[0, 1, 1])
     prepare(wf0, u_ref[0, 0, 0], -u_ref[0, 0, 1])
@@ -195,7 +210,7 @@
         tmp[rows, :] = -lower - times(upper, wc.at[y], False)
 
     tiles(width, tall, backward_map)
-    pass_on()
+    pass_on(c_all, sem_c)
     prepare(wh, tmp[:width, :width], tmp[:width, width:])
 
     def local_ends(i):
@@ -204,19 +219,10 @@
 
     tiles(vectors, tall, local_ends)
 
-    land(half_of(after, 1), sem_c, 1, left)
-    prepare(wc.at[after], c_all[after, :, :width], c_all[after, :, width:])
-    if ysize > 2:
-        land(half_of(ahead_y, 0), sem_c, 3, right)
-        prepare(wc.at[ahead_y], c_all[ahead_y, :, :width], c_all[ahead_y, :, width:])
-        far = lax.rem(y + 2, ysize)
-        land(half_of(far, 0), sem_c, 4, left)
-        land(half_of(far, 1), sem_c, 5, right)
-        prepare(wc.at[far], c_all[far, :, :width], c_all[far, :, width:])
+    take(c_all, sem_c, wc)
     for d in order:
         land(b_all.at[back(y, d, ysize)], sem_b, d, along("y", y, ysize - d, ysize))
-    for d in order:
-        go(d_all.at[y], d_all.at[y], sem_d, d, along("y", y, d, ysize))
+    share(d_all, sem_d)
 
     value = b_all[0]
     for k in range(1, ysize):
@@ -245,6 +251,9 @@
         tiles(width, tall, group_forward)
         prepare(wp, tmp[:width, :width], tmp[:width, width:])
 
+    early = z < 3
+    pl.when(jnp.logical_not(early))(lambda: pass_on(d_all, sem_d))
+
     for s in range(SUBS):
         rows = pl.ds(s * sub, sub)
 
@@ -268,8 +277,8 @@
         def _():
             remote(staging.at[k], piece(into, y), sems, k, y, {"y": k}).start()
 
-    def handed_out(staging, into, sems):
-        for k in range(ysize):
+    def handed_out(staging, into, sems, count):
+        for k in range(count):
             @pl.when(y != k)
             def _():
                 remote(staging.at[k], piece(into, y), sems, k, y, {"y": k}).wait_send()
@@ -280,11 +289,7 @@
         if k < ysize - 1:
             value = times(value, wc.at[k], True) + b_all[k]
 
-    prepare(wd.at[y], d_all[y, :, :width], d_all[y, :, width:])
-    for d in order:
-        k = back(y, d, ysize)
-        land(d_all.at[k], sem_d, d, along("y", y, ysize - d, ysize))
-        prepare(wd.at[k], d_all[k, :, :width], d_all[k, :, width:])
+    pl.when(early)(lambda: pass_on(d_all, sem_d))
 
     for d in [0] + order:
         j = lax.rem(y + d, ysize)
@@ -298,6 +303,32 @@
         else:
             e_all[y] = ends
 
+    prepare(wd.at[y], d_all[y, :, :width], d_all[y, :, width:])
+    take(d_all, sem_d, wd)
+    even = lax.rem(z, 2) == 0
+    jumps = jnp.logical_and(even, jnp.logical_and(z >= 2, z <= zsize - 4))
+    feeds = jnp.logical_and(jnp.logical_not(even), z <= zsize - 5)
+    leaps = jnp.logical_and(even, z <= zsize - 6)
+    last = z == zsize - 1
+    inner = jnp.logical_and(z > 0, z < zsize - 1)
+    steps = jnp.logical_and(inner, z >= zsize - 3)
+
+    @pl.when(inner)
+    def _():
+        def compose(i):
+            value = d_all[0, pl.ds(i, tall), :]
+            for k in range(1, ysize):
+                value = times(value, wd.at[k], False)
+            dg[pl.ds(i, tall), :] = value
+
+        tiles(width, tall, compose)
+
+    @pl.when(feeds)
+    def _():
+        remote(dg, dz, sem_one, 0, 0, ahead).start()
+
+    pl.when(inner)(lambda: prepare(wq, dg[:, :width], dg[:, width:]))
+
     def swept(i):
         rows = pl.ds(i, tall)
         value = vin[rows, :]
@@ -306,48 +337,124 @@
 
     tiles(vectors, tall, swept)
 
-    @pl.when(jnp.logical_and(z > 0, z < zsize - 1))
-    def _():
-        def compose(i):
-            value = d_all[0, pl.ds(i, tall), :]
-            for k in range(1, ysize):
-                value = times(value, wd.at[k], False)
-            tmp[pl.ds(i, tall), :] = value
-
-        tiles(width, tall, compose)
-        prepare(wq, tmp[:width, :width], tmp[:width, width:])
-
     for d in order:
         j = lax.rem(y + d, ysize)
         remote(e_all.at[j], e_all.at[j], sem_e, j, j, {"y": j}).wait_recv()
-    value = e_all[ysize - 1]
+    values = [e_all[ysize - 1]]
     for k in reversed(range(ysize - 1)):
-        value = times(value, wd.at[k], True) + e_all[k]
-    rg[...] = value
-
-    @pl.when(z == zsize - 1)
+        values.append(times(values[-1], wd.at[k], True) + e_all[k])
+    rg[...] = values[-1]
+
+    @pl.when(last)
     def _():
         for s in range(SUBS):
             hop(rg, wz, sem_bz, s, behind).start()
         wz[...] = jnp.zeros_like(wz)
 
+    @pl.when(feeds)
+    def _():
+        remote(rg, rz, sem_one, 1, 1, ahead).start()
+
+    for k in range(ysize - 1):
+        hand_out(k, values[ysize - 2 - k], wk, win, sem_r)
+
+    @pl.when(jumps)
+    def _():
+        remote(dz, dz, sem_one, 0, 0, behind).wait_recv()
+        prepare(wz1, dz[:, :width], dz[:, width:])
+
+        def joint(i):
+            tmp[pl.ds(i, tall), :] = times(dz[pl.ds(i, tall), :], wq, False)
+
+        tiles(width, tall, joint)
+        prepare(wj, tmp[:width, :width], tmp[:width, width:])
+        remote(rz, rz, sem_one, 1, 1, behind).wait_recv()
+        rj[...] = times(rg[...], wz1, True) + rz[...]
+
+    def settle():
+        @pl.when(y < ysize - 1)
+        def _():
+            for d in order:
+                j = lax.rem(y + d, ysize)
+                remote(piece(win, j), piece(win, j), sem_r, j, j, {"y": j}).wait_recv()
+
+            def inner_part(i):
+                rows = pl.ds(i, tall)
+                y1[rows, :] = y1[rows, :] - times(win[rows, :], wf1, True)
+
+            tiles(vectors, tall, inner_part)
+
+        def first_part(i):
+            rows = pl.ds(i, tall)
+            y0[rows, :] = y0[rows, :] - times(y1[rows, :], wf0, True)
+
+        tiles(vectors, tall, first_part)
+
+        @pl.when(z < zsize - 1)
+        def _():
+            am[:, :width] = u_ref[0, 1, 0]
+            am[:, width:] = -u_ref[0, 1, 1]
+            for k in range(1, ysize):
+                @pl.when(k > y)
+                def _():
+                    def longer(i):
+                        am[pl.ds(i, tall), :] = times(am[pl.ds(i, tall), :], wd.at[k], False)
+
+                    tiles(width, tall, longer)
+            prepare(wa1, am[:, :width], am[:, width:])
+
+            def both(i):
+                rows = pl.ds(i, tall)
+                upper = jnp.concatenate([u_ref[0, 0, 0, rows, :], -u_ref[0, 0, 1, rows, :]], axis=1)
+                am[rows, :] = times(upper, wa1, False)
+
+            tiles(width, tall, both)
+            prepare(wa0, am[:, :width], am[:, width:])
+
+    soon = z >= zsize // 2
+    pl.when(jnp.logical_not(soon))(settle)
+
+    two_on, two_back = along("z", z, 2, zsize), along("z", z, zsize - 2, zsize)
+
+    def spread(s, k):
+        rows = pl.ds(pl.multiple_of(y * chunk + s * sub, sub), sub)
+        return remote(
+            wz.at[pl.ds(s * sub, sub), :], wb.at[rows, :], sem_w, k * SUBS + s, y * SUBS + s, {"y": k}
+        )
+
     for s in range(SUBS):
         rows = pl.ds(s * sub, sub)
 
-        @pl.when(z < zsize - 1)
+        @pl.when(leaps)
+        def _():
+            hop(wz, wz, sem_far, s, two_on).wait_recv()
+
+        @pl.when(jnp.logical_and(z < zsize - 1, jnp.logical_not(leaps)))
         def _():
             hop(wz, wz, sem_bz, s, ahead).wait_recv()
 
-        @pl.when(jnp.logical_and(z > 0, z < zsize - 1))
+        @pl.when(steps)
         def _():
             wo[rows, :] = times(wz[rows, :], wq, True) + rg[rows, :]
             hop(wo, wz, sem_bz, s, behind).start()
 
-    value = wz[...]
-    for k in reversed(range(ysize)):
-        hand_out(k, value, wk, win, sem_w)
-        if k > 0:
-            value = times(value, wd.at[k], True) + e_all[k]
+        @pl.when(jumps)
+        def _():
+            rj[rows, :] = times(wz[rows, :], wj, True) + rj[rows, :]
+            hop(rj, wz, sem_far, s, two_back).start()
+
+        @pl.when(z < zsize - 1)
+        def _():
+            for d in order:
+                spread(s, lax.rem(y + d, ysize)).start()
+
+    @pl.when(jumps)
+    def _():
+        wo[...] = times(wz[...], wq, True) + rg[...]
+        for s in range(SUBS):
+            hop(wo, wz, sem_bz, s, behind).start()
+
+    pl.when(soon)(settle)
 
     sibling = {"core": 1 - core}
     wreal, wimag = w_ref[0, 0], w_ref[0, 1]
@@ -377,12 +484,23 @@
     turns = [0] + order
     for turn, d in enumerate(turns):
         j, rows = rows_of(d)
-        if d:
-            remote(win.at[rows, :], win.at[rows, :], sem_w, j, j, {"y": j}).wait_recv()
-        second = y1[rows, :] - times(win[rows, :], wf1, True)
-        first = y0[rows, :] - times(second, wf0, True)
-        for n, solved in enumerate((first, second)):
-            real, imag = solved[:, :width], solved[:, width:]
+
+        @pl.when(z < zsize - 1)
+        def _():
+            if d:
+                for s in range(SUBS):
+                    part_rows = pl.ds(pl.multiple_of(j * chunk + s * sub, sub), sub)
+                    remote(
+                        wb.at[part_rows, :], wb.at[part_rows, :], sem_w, j * SUBS + s, j * SUBS + s, {"y": j}
+                    ).wait_recv()
+                inflow = wb[rows, :]
+            else:
+                inflow = wz[...]
+            y1[rows, :] = y1[rows, :] - times(inflow, wa1, True)
+            y0[rows, :] = y0[rows, :] + times(inflow, wa0, True)
+
+        for n, solved in enumerate((y0, y1)):
+            real, imag = solved[rows, :width], solved[rows, width:]
             xs[n, rows, :width] = wreal * real - wimag * imag
             xs[n, rows, width:] = wreal * imag + wimag * real
         go(xs.at[1 - core, rows, :], other.at[rows, :], sem_a, turn, sibling)
@@ -492,8 +610,11 @@
     out_ref[1] = jnp.concatenate([fin[k][:, part:] for k in slots], axis=1)
     for copy in sent:
         copy.wait_send()
-    handed_out(vk, vin, sem_v)
-    handed_out(wk, win, sem_w)
+    if ysize > 2:
+        for copy in (*onward(c_all, sem_c), *onward(d_all, sem_d)):
+            copy.wait_send()
+    handed_out(vk, vin, sem_v, ysize)
+    handed_out(wk, win, sem_r, ysize - 1)
     for d in order:
         j, rows = rows_of(d)
         remote(eo.at[rows, :], e_all.at[y], sem_e, j, y, {"y": j}).wait_send()
@@ -502,9 +623,23 @@
         def _():
             hop(vo, vz, sem_fz, s, ahead).wait_send()
 
-        @pl.when(z > 0)
+        @pl.when(jnp.logical_or(last, jnp.logical_or(steps, jumps)))
         def _():
             hop(wo, wz, sem_bz, s, behind).wait_send()
+
+        @pl.when(jumps)
+        def _():
+            hop(rj, wz, sem_far, s, two_back).wait_send()
+
+        @pl.when(z < zsize - 1)
+        def _():
+            for d in order:
+                spread(s, lax.rem(y + d, ysize)).wait_send()
+
+    @pl.when(feeds)
+    def _():
+        remote(dg, dz, sem_one, 0, 0, ahead).wait_send()
+        remote(rg, rz, sem_one, 1, 1, ahead).wait_send()
 
 
 def shards(sizes, subspace, pivots, lower_blocks, upper_blocks, pole_weights):
@@ -537,11 +672,12 @@
         + [prepared()] * 4
         + [prepared(2)]
         + [prepared(ysize)] * 2
-        + [prepared()] * 3
+        + [prepared()] * 7
         + [f32(ysize, width, wide)] * 2
         + [f32(ysize, chunk, wide)] * 2
-        + [f32(chunk, wide)] * 2
-        + [f32(vectors, wide)] * 9
+        + [f32(chunk, wide)] * 4
+        + [f32(vectors, wide)] * 10
+        + [f32(width, wide)] * 3
         + [f32(chunk, wide)] * 4
         + [f32(ysize, chunk, wide)] * 2
         + [
@@ -564,8 +700,11 @@
             pltpu.SemaphoreType.DMA((4,)),
             dma(6),
         ]
-        + [dma(ysize)] * 5
+        + [dma(ysize), dma(6)]
+        + [dma(ysize)] * 3
+        + [dma(ysize * SUBS)]
         + [dma(SUBS)] * 2
+        + [dma(2), dma(SUBS)]
         + [
             dma(ysize),
             dma(ysize * xsize),

time: 149 us -> 144 us (0.966)
  Pallas kernels: 147 us -> 142 us
    pallas_call x1, Pallas kernels: 147 us -> 142 us  [shards(): pl.pallas_call(functools.partial(step_kernel, (xsize, zsize, ysize), tota...]
where the time goes in v3:
time: 144 us
  Pallas kernels  142 us (99%)
  local copies, waits for them, and re-layouts  1.57 us (1%)
    pallas_call x1, Pallas kernels, shards(): pl.pallas_call(functools.partial(step_kernel, (xsize, zsize, ysize), tota...  142 us

profile of v3, /device:TPU:1, one launch (start us, length us, event | category | flops | bytes accessed | tf_op | source)
XLA Modules:
  0.0 143.7 jit_solution(4935682757963371769)
XLA Ops:
  0.0 142.1 %step.1 = f32[2,32,512]{2,1,0:T(8,128)} custom-call(f32[2,256,512]{2,1,0:T(8,128)} %f_hbm.1, f32[1,2,2,256,256]{4,3,2,1,0:T(8,128)} %g_hbm.1, f32[1,2,2,256,256]{4,3,2,1,0:T(8,128)} %e_hbm.1, f32[1,2,2,256,256]{4,3,2,1,0:T(8,128)} %u_hbm.1, f32[1,2]{1,0:T(1,128)} %w_ref.1), custom_call_target="tpu_custom_call" | custom-call | tf_op jit(solution)/shard_map/step/pallas_call | solution.py:666
  142.1 1.6 %copy.7 = f32[2,32,512]{2,1,0:T(8,128)} copy(f32[2,32,512]{2,1,0:T(8,128)} %step.1) | data formatting | bytes 262144

commit v4 on v3

--- a/solution.py
+++ b/solution.py
@@ -33,12 +33,12 @@
 
 
 def prepare(weights, real, minus):
-    size = real.shape[0]
+    height, width = real.shape
     for part, (r, m) in enumerate(zip(halves(real), halves(minus))):
-        weights[part, :size, :size] = r
-        weights[part, :size, size:] = m
-        weights[part, size:, :size] = -m
-        weights[part, size:, size:] = r
+        weights[part, :height, :width] = r
+        weights[part, :height, width:] = m
+        weights[part, height:, :width] = -m
+        weights[part, height:, width:] = r
 
 
 def tiles(count, size, body):
@@ -74,9 +74,9 @@
     we0, we1, wf0, wf1, wg, wc, wd, wp, wq, wh, wj, wz1, wa0, wa1,
     c_all, d_all, b_all, e_all, qg, rg, rj, rz, s0, s1, y0, y1, e0, eo, vin, win, tmp, wb, dg, dz, am,
     vz, vo, wz, wo, vk, wk,
-    xs, other, cut, got, gram, g1, t1, g2, g3, h2, h1, wn, zs, turned, spun, fin,
+    xs, other, cut, got, gram, g1, t1, g2, g3, h2, h1, wn, zs, turned, qall,
     sem_in, sem_c, sem_b, sem_d, sem_v, sem_e, sem_r, sem_w, sem_fz, sem_bz, sem_one, sem_far,
-    sem_a, sem_x, sem_1, sem_2, sem_3, sem_4, sem_5, sem_6,
+    sem_a, sem_x, sem_1, sem_2, sem_3, sem_4, sem_5, sem_q,
 ):
     xsize, zsize, ysize = dims
     x, core, z, y = (lax.axis_index(a) for a in AXES)
@@ -249,7 +249,7 @@
             tmp[pl.ds(i, tall), :] = value
 
         tiles(width, tall, group_forward)
-        prepare(wp, tmp[:width, :width], tmp[:width, width:])
+        prepare(wp, tmp[:width, :width].T, -tmp[:width, width:].T)
 
     early = z < 3
     pl.when(jnp.logical_not(early))(lambda: pass_on(d_all, sem_d))
@@ -263,7 +263,7 @@
 
         @pl.when(jnp.logical_and(z > 0, z < zsize - 1))
         def _():
-            vo[rows, :] = times(vz[rows, :], wp, True) + qg[rows, :]
+            vo[rows, :] = times(vz[rows, :], wp, False) + qg[rows, :]
             hop(vo, vz, sem_fz, s, ahead).start()
 
     def hand_out(k, value, staging, into, sems):
@@ -327,7 +327,8 @@
     def _():
         remote(dg, dz, sem_one, 0, 0, ahead).start()
 
-    pl.when(inner)(lambda: prepare(wq, dg[:, :width], dg[:, width:]))
+    pl.when(jumps)(lambda: prepare(wq, dg[:, :width], dg[:, width:]))
+    pl.when(steps)(lambda: prepare(wq, dg[:, :width].T, -dg[:, width:].T))
 
     def swept(i):
         rows = pl.ds(i, tall)
@@ -367,7 +368,7 @@
             tmp[pl.ds(i, tall), :] = times(dz[pl.ds(i, tall), :], wq, False)
 
         tiles(width, tall, joint)
-        prepare(wj, tmp[:width, :width], tmp[:width, width:])
+        prepare(wj, tmp[:width, :width].T, -tmp[:width, width:].T)
         remote(rz, rz, sem_one, 1, 1, behind).wait_recv()
         rj[...] = times(rg[...], wz1, True) + rz[...]
 
@@ -435,12 +436,12 @@
 
         @pl.when(steps)
         def _():
-            wo[rows, :] = times(wz[rows, :], wq, True) + rg[rows, :]
+            wo[rows, :] = times(wz[rows, :], wq, False) + rg[rows, :]
             hop(wo, wz, sem_bz, s, behind).start()
 
         @pl.when(jumps)
         def _():
-            rj[rows, :] = times(wz[rows, :], wj, True) + rj[rows, :]
+            rj[rows, :] = times(wz[rows, :], wj, False) + rj[rows, :]
             hop(rj, wz, sem_far, s, two_back).start()
 
         @pl.when(z < zsize - 1)
@@ -515,19 +516,29 @@
     basis = got[0]
     for j in range(1, xsize):
         basis = basis + got[j]
-    real, imag = basis[:, :part], basis[:, part:]
-    lh, ll = halves(basis)
-    rh, rl = halves(jnp.concatenate([real + imag, imag - real], axis=1))
+    qall[core, x] = basis
+    go(qall.at[core, x], qall.at[core, x], sem_q, 0, sibling)
+    land(qall.at[1 - core, x], sem_q, 0, sibling)
+    low_rows = pl.ds(pl.multiple_of(core * (vectors // 2), vectors // 2), vectors // 2)
+    left_side = jnp.concatenate([qall[n, x, low_rows, :] for n in range(2)], axis=1)
+    right_side = []
+    for n in range(2):
+        real, imag = qall[n, x, :, :part], qall[n, x, :, part:]
+        right_side += [real + imag, imag - real]
+    lh, ll = halves(left_side)
+    rh, rl = halves(jnp.concatenate(right_side, axis=1))
     gram[...] = dot(lh, rh, True) + dot(ll, rh, True) + dot(lh, rl, True)
-
-    for d in range(1, poles):
-        p, device = pole_of(d)
-        go(lines(gram, p, own), g1.at[pole], sem_1, d, device)
-    g1[pole] = lines(gram, pole, own)[...]
-    for d in range(1, poles):
-        land(g1.at[back(pole, d, poles)], sem_1, d, pole_of(poles - d)[1])
+    for step in nearest_first(xsize):
+        j = lax.rem(x + step, xsize)
+        go(lines(gram, j, own), g1.at[x], sem_1, step, {"x": j})
+    g1[x] = lines(gram, x, own)[...]
+    for step in nearest_first(xsize):
+        go(qall.at[core, x], qall.at[core, x], sem_q, step, along("x", x, step, xsize))
+    for step in nearest_first(xsize):
+        j = back(x, step, xsize)
+        land(g1.at[j], sem_1, step, {"x": j})
     value = g1[0]
-    for j in range(1, poles):
+    for j in range(1, xsize):
         value = value + g1[j]
     t1[...] = value
     for d in nearest_first(ysize):
@@ -555,11 +566,24 @@
     for d in nearest_first(ysize):
         j = back(y, d, ysize)
         land(lines(h2, j, line), sem_4, d, {"y": j})
-    lines(h1, pole, own)[...] = h2[...]
+    place = core * xsize + x
+    lines(h1, place, own)[...] = h2[...]
     for d in range(1, poles):
-        go(h2, lines(h1, pole, own), sem_5, d, pole_of(d)[1])
+        go(h2, lines(h1, place, own), sem_5, d, pole_of(d)[1])
+    for step in nearest_first(xsize):
+        j = back(x, step, xsize)
+        land(qall.at[core, j], sem_q, step, {"x": j})
+        go(qall.at[core, j], qall.at[core, j], sem_q, xsize + step, sibling)
+    for step in nearest_first(xsize):
+        land(qall.at[1 - core, back(x, step, xsize)], sem_q, xsize + step, sibling)
+    prepare(
+        turned,
+        jnp.concatenate([qall[n, j, :, :part] for n in range(2) for j in range(xsize)], axis=1),
+        jnp.concatenate([qall[n, j, :, part:] for n in range(2) for j in range(xsize)], axis=1),
+    )
     for d in range(1, poles):
-        land(lines(h1, back(pole, d, poles), own), sem_5, d, pole_of(poles - d)[1])
+        p, device = pole_of(poles - d)
+        land(lines(h1, lax.rem(p, 2) * xsize + p // 2, own), sem_5, d, device)
 
     whole = h1[...]
     frob = jnp.sqrt(jnp.sum(whole * whole))
@@ -586,28 +610,11 @@
         zs[1, :, vectors:] - 1.5 * zs[0, :, vectors:],
     )
     size = jnp.sqrt(total_rows / frob)
-    stacked = jnp.concatenate(
-        [basis, jnp.concatenate([-imag, real], axis=1)], axis=0
-    )
-    qh, ql = halves(stacked)
-    turned[0] = qh
-    turned[1] = ql
-
-    def rotate(i):
-        rows = pl.ds(i, tall)
-        mix = 1.5 * zs[0, rows, :] + times(zs[1, rows, :], wn.at[1], False)
-        spun[rows, :] = times(mix, turned, False) * size
-
-    tiles(vectors, tall, rotate)
-    for d in range(1, poles):
-        p, device = pole_of(d)
-        go(lines(spun, p, own), fin.at[pole], sem_6, d, device)
-    fin[pole] = lines(spun, pole, own)[...]
-    for d in range(1, poles):
-        land(fin.at[back(pole, d, poles)], sem_6, d, pole_of(poles - d)[1])
-    slots = [2 * j + n for n in range(2) for j in range(xsize)]
-    out_ref[0] = jnp.concatenate([fin[k][:, :part] for k in slots], axis=1)
-    out_ref[1] = jnp.concatenate([fin[k][:, part:] for k in slots], axis=1)
+    rows = pl.ds(pl.multiple_of(pole * own, own), own)
+    mix = 1.5 * zs[0, rows, :] + times(zs[1, rows, :], wn.at[1], False)
+    turned_rows = times(mix, turned, False) * size
+    out_ref[0] = turned_rows[:, : 2 * width]
+    out_ref[1] = turned_rows[:, 2 * width :]
     for copy in sent:
         copy.wait_send()
     if ysize > 2:
@@ -685,8 +692,8 @@
             f32(vectors, wide),
             f32(xsize, vectors, 2 * part),
             f32(xsize, vectors, 2 * part),
-            f32(vectors, vectors),
-            f32(poles, own, vectors),
+            f32(vectors // 2, vectors),
+            f32(xsize, own, vectors),
             f32(own, vectors),
             f32(ysize, line, vectors),
             f32(zsize, line, vectors),
@@ -694,9 +701,8 @@
             f32(vectors, vectors),
             pltpu.VMEM((2, 2, 2 * vectors, 2 * vectors), BF16),
             f32(2, vectors, 2 * vectors),
-            pltpu.VMEM((2, 2 * vectors, 2 * part), BF16),
-            f32(vectors, 2 * part),
-            f32(poles, own, 2 * part),
+            pltpu.VMEM((2, 2 * vectors, 2 * wide), BF16),
+            f32(2, xsize, vectors, 2 * part),
             pltpu.SemaphoreType.DMA((4,)),
             dma(6),
         ]
@@ -708,12 +714,12 @@
         + [
             dma(ysize),
             dma(ysize * xsize),
-            dma(poles),
+            dma(xsize),
             dma(ysize),
             dma(zsize),
             dma(ysize),
             dma(poles),
-            dma(poles),
+            dma(2 * xsize),
         ],
         compiler_params=pltpu.CompilerParams(
             collective_id=0, has_side_effects=True, vmem_limit_bytes=60 * 2**20

time: 144 us -> 139 us (0.965)
  Pallas kernels: 142 us -> 137 us
    pallas_call x1, Pallas kernels: 142 us -> 137 us  [shards(): pl.pallas_call(functools.partial(step_kernel, (xsize, zsize, ysize), tota...]
where the time goes in v4:
time: 139 us; the launch traced here: 138 us
  Pallas kernels  137 us (99%)
  local copies, waits for them, and re-layouts  1.57 us (1%)
    pallas_call x1, Pallas kernels, shards(): pl.pallas_call(functools.partial(step_kernel, (xsize, zsize, ysize), tota...  137 us

profile of v4, /device:TPU:1, one launch (start us, length us, event | category | flops | bytes accessed | tf_op | source)
XLA Modules:
  0.0 138.4 jit_solution(6510243503071907810)
XLA Ops:
  0.0 136.8 %step.1 = f32[2,32,512]{2,1,0:T(8,128)} custom-call(f32[2,256,512]{2,1,0:T(8,128)} %f_hbm.1, f32[1,2,2,256,256]{4,3,2,1,0:T(8,128)} %g_hbm.1, f32[1,2,2,256,256]{4,3,2,1,0:T(8,128)} %e_hbm.1, f32[1,2,2,256,256]{4,3,2,1,0:T(8,128)} %u_hbm.1, f32[1,2]{1,0:T(1,128)} %w_ref.1), custom_call_target="tpu_custom_call" | custom-call | tf_op jit(solution)/shard_map/step/pallas_call | solution.py:673
  136.8 1.6 %copy.7 = f32[2,32,512]{2,1,0:T(8,128)} copy(f32[2,32,512]{2,1,0:T(8,128)} %step.1) | data formatting | bytes 262144

commit v5 on v4

--- a/solution.py
+++ b/solution.py
@@ -74,9 +74,9 @@
     we0, we1, wf0, wf1, wg, wc, wd, wp, wq, wh, wj, wz1, wa0, wa1,
     c_all, d_all, b_all, e_all, qg, rg, rj, rz, s0, s1, y0, y1, e0, eo, vin, win, tmp, wb, dg, dz, am,
     vz, vo, wz, wo, vk, wk,
-    xs, other, cut, got, gram, g1, t1, g2, g3, h2, h1, wn, zs, turned, qall,
+    xs, other, cut, got, gram, g1, g3, h1, wn, zs, turned, qall,
     sem_in, sem_c, sem_b, sem_d, sem_v, sem_e, sem_r, sem_w, sem_fz, sem_bz, sem_one, sem_far,
-    sem_a, sem_x, sem_1, sem_2, sem_3, sem_4, sem_5, sem_q,
+    sem_a, sem_x, sem_1, sem_3, sem_5, sem_q,
 ):
     xsize, zsize, ysize = dims
     x, core, z, y = (lax.axis_index(a) for a in AXES)
@@ -99,12 +99,13 @@
         return {axis: lax.rem(me + d, size)}
 
     barrier = pltpu.get_barrier_semaphore()
-    for d in range(1, ysize):
-        pl.semaphore_signal(barrier, inc=1, device_id=along("y", y, d, ysize), device_id_type=MESH_ID)
+    for dp in range(poles):
+        for dy in range(ysize):
+            if dp or dy:
+                device = pole_of(dp)[1] | along("y", y, dy, ysize)
+                pl.semaphore_signal(barrier, inc=1, device_id=device, device_id_type=MESH_ID)
     for d in range(1, zsize):
         pl.semaphore_signal(barrier, inc=1, device_id=along("z", z, d, zsize), device_id_type=MESH_ID)
-    for d in range(1, poles):
-        pl.semaphore_signal(barrier, inc=1, device_id=pole_of(d)[1], device_id_type=MESH_ID)
 
     loads = [
         pltpu.make_async_copy(a, b, sem_in.at[i])
@@ -140,7 +141,7 @@
         c_all[y, pl.ds(i, tall), :] = times(rows, we0, False)
 
     tiles(width, tall, forward_map)
-    pl.semaphore_wait(barrier, ysize + zsize + poles - 3)
+    pl.semaphore_wait(barrier, ysize * poles + zsize - 2)
 
     half = width // 2
     right, left = along("y", y, 1, ysize), along("y", y, ysize - 1, ysize)
@@ -528,29 +529,22 @@
     lh, ll = halves(left_side)
     rh, rl = halves(jnp.concatenate(right_side, axis=1))
     gram[...] = dot(lh, rh, True) + dot(ll, rh, True) + dot(lh, rl, True)
-    for step in nearest_first(xsize):
-        j = lax.rem(x + step, xsize)
-        go(lines(gram, j, own), g1.at[x], sem_1, step, {"x": j})
-    g1[x] = lines(gram, x, own)[...]
+    plane = [(dx, dy) for dx in range(xsize) for dy in range(ysize) if dx or dy]
+    plane.sort(key=lambda p: min(p[0], xsize - p[0]) + min(p[1], ysize - p[1]))
+    here = x * ysize + y
+    for dx, dy in plane:
+        slot = dx * ysize + dy
+        jx, jy = lax.rem(x + dx, xsize), lax.rem(y + dy, ysize)
+        go(lines(gram, jx * ysize + jy, line), g1.at[here], sem_1, slot, {"x": jx, "y": jy})
+    g1[here] = lines(gram, here, line)[...]
     for step in nearest_first(xsize):
         go(qall.at[core, x], qall.at[core, x], sem_q, step, along("x", x, step, xsize))
-    for step in nearest_first(xsize):
-        j = back(x, step, xsize)
-        land(g1.at[j], sem_1, step, {"x": j})
+    for dx, dy in plane:
+        jx, jy = back(x, dx, xsize), back(y, dy, ysize)
+        land(g1.at[jx * ysize + jy], sem_1, dx * ysize + dy, {"x": jx, "y": jy})
     value = g1[0]
-    for j in range(1, xsize):
+    for j in range(1, xsize * ysize):
         value = value + g1[j]
-    t1[...] = value
-    for d in nearest_first(ysize):
-        j = lax.rem(y + d, ysize)
-        go(lines(t1, j, line), g2.at[y], sem_2, d, {"y": j})
-    g2[y] = lines(t1, y, line)[...]
-    for d in nearest_first(ysize):
-        j = back(y, d, ysize)
-        land(g2.at[j], sem_2, d, {"y": j})
-    value = g2[0]
-    for j in range(1, ysize):
-        value = value + g2[j]
     g3[z] = value
     for d in nearest_first(zsize):
         go(g3.at[z], g3.at[z], sem_3, d, {"z": lax.rem(z + d, zsize)})
@@ -560,16 +554,12 @@
     value = g3[0]
     for j in range(1, zsize):
         value = value + g3[j]
-    lines(h2, y, line)[...] = value
-    for d in nearest_first(ysize):
-        go(lines(h2, y, line), lines(h2, y, line), sem_4, d, {"y": lax.rem(y + d, ysize)})
-    for d in nearest_first(ysize):
-        j = back(y, d, ysize)
-        land(lines(h2, j, line), sem_4, d, {"y": j})
-    place = core * xsize + x
-    lines(h1, place, own)[...] = h2[...]
-    for d in range(1, poles):
-        go(h2, lines(h1, place, own), sem_5, d, pole_of(d)[1])
+    place = (core * xsize + x) * ysize + y
+    lines(h1, place, line)[...] = value
+    others = [(dp, dy) for dp in range(poles) for dy in range(ysize) if dp or dy]
+    for dp, dy in others:
+        device = pole_of(dp)[1] | along("y", y, dy, ysize)
+        go(lines(h1, place, line), lines(h1, place, line), sem_5, dp * ysize + dy, device)
     for step in nearest_first(xsize):
         j = back(x, step, xsize)
         land(qall.at[core, j], sem_q, step, {"x": j})
@@ -581,9 +571,11 @@
         jnp.concatenate([qall[n, j, :, :part] for n in range(2) for j in range(xsize)], axis=1),
         jnp.concatenate([qall[n, j, :, part:] for n in range(2) for j in range(xsize)], axis=1),
     )
-    for d in range(1, poles):
-        p, device = pole_of(poles - d)
-        land(lines(h1, lax.rem(p, 2) * xsize + p // 2, own), sem_5, d, device)
+    for dp, dy in others:
+        p, device = pole_of(poles - dp)
+        jy = back(y, dy, ysize)
+        source = (lax.rem(p, 2) * xsize + p // 2) * ysize + jy
+        land(lines(h1, source, line), sem_5, dp * ysize + dy, device | {"y": jy})
 
     whole = h1[...]
     frob = jnp.sqrt(jnp.sum(whole * whole))
@@ -693,11 +685,8 @@
             f32(xsize, vectors, 2 * part),
             f32(xsize, vectors, 2 * part),
             f32(vectors // 2, vectors),
-            f32(xsize, own, vectors),
-            f32(own, vectors),
-            f32(ysize, line, vectors),
+            f32(xsize * ysize, line, vectors),
             f32(zsize, line, vectors),
-            f32(own, vectors),
             f32(vectors, vectors),
             pltpu.VMEM((2, 2, 2 * vectors, 2 * vectors), BF16),
             f32(2, vectors, 2 * vectors),
@@ -714,11 +703,9 @@
         + [
             dma(ysize),
             dma(ysize * xsize),
-            dma(xsize),
-            dma(ysize),
+            dma(xsize * ysize),
             dma(zsize),
-            dma(ysize),
-            dma(poles),
+            dma(poles * ysize),
             dma(2 * xsize),
         ],
         compiler_params=pltpu.CompilerParams(

time: 139 us -> 135 us (0.971)
  Pallas kernels: 137 us -> 133 us
    pallas_call x1, Pallas kernels: 137 us -> 133 us  [shards(): pl.pallas_call(functools.partial(step_kernel, (xsize, zsize, ysize), tota...]
where the time goes in v5:
time: 135 us
  Pallas kernels  133 us (99%)
  local copies, waits for them, and re-layouts  1.57 us (1%)
    pallas_call x1, Pallas kernels, shards(): pl.pallas_call(functools.partial(step_kernel, (xsize, zsize, ysize), tota...  133 us

profile of v5, /device:TPU:1, one launch (start us, length us, event | category | flops | bytes accessed | tf_op | source)
XLA Modules:
  0.0 134.7 jit_solution(11933692209828172831)
XLA Ops:
  0.0 133.1 %step.1 = f32[2,32,512]{2,1,0:T(8,128)} custom-call(f32[2,256,512]{2,1,0:T(8,128)} %f_hbm.1, f32[1,2,2,256,256]{4,3,2,1,0:T(8,128)} %g_hbm.1, f32[1,2,2,256,256]{4,3,2,1,0:T(8,128)} %e_hbm.1, f32[1,2,2,256,256]{4,3,2,1,0:T(8,128)} %u_hbm.1, f32[1,2]{1,0:T(1,128)} %w_ref.1), custom_call_target="tpu_custom_call" | custom-call | tf_op jit(solution)/shard_map/step/pallas_call | solution.py:665
  133.2 1.6 %copy.7 = f32[2,32,512]{2,1,0:T(8,128)} copy(f32[2,32,512]{2,1,0:T(8,128)} %step.1) | data formatting | bytes 262144

commit v6 on v5

--- a/solution.py
+++ b/solution.py
@@ -72,10 +72,10 @@
     dims, total_rows, f_hbm, g_hbm, e_hbm, u_hbm, w_ref, out_ref,
     f_ref, g_ref, e_ref, u_ref,
     we0, we1, wf0, wf1, wg, wc, wd, wp, wq, wh, wj, wz1, wa0, wa1,
-    c_all, d_all, b_all, e_all, qg, rg, rj, rz, s0, s1, y0, y1, e0, eo, vin, win, tmp, wb, dg, dz, am,
+    c_all, d_all, b_all, e_all, qg, rg, rj, rz, s0, s1, y0, y1, e0, eo, vin, win, tmp, wb, dg, dz, am, cg,
     vz, vo, wz, wo, vk, wk,
     xs, other, cut, got, gram, g1, g3, h1, wn, zs, turned, qall,
-    sem_in, sem_c, sem_b, sem_d, sem_v, sem_e, sem_r, sem_w, sem_fz, sem_bz, sem_one, sem_far,
+    sem_in, sem_c, sem_b, sem_d, sem_v, sem_e, sem_r, sem_w, sem_fz, sem_bz, sem_one, sem_far, sem_skip,
     sem_a, sem_x, sem_1, sem_3, sem_5, sem_q,
 ):
     xsize, zsize, ysize = dims
@@ -212,7 +212,7 @@
 
     tiles(width, tall, backward_map)
     pass_on(c_all, sem_c)
-    prepare(wh, tmp[:width, :width], tmp[:width, width:])
+    prepare(wh, tmp[:width, :width].T, -tmp[:width, width:].T)
 
     def local_ends(i):
         rows = pl.ds(i, tall)
@@ -235,6 +235,11 @@
 
     ahead, behind = along("z", z, 1, zsize), along("z", z, zsize - 1, zsize)
 
+    skips = z == (zsize - 3 if zsize > 3 else -1)
+    lends = z == (zsize - 2 if zsize > 3 else -1)
+    served = z == (zsize - 1 if zsize > 3 else -1)
+    two_on, two_back = along("z", z, 2, zsize), along("z", z, zsize - 2, zsize)
+
     @pl.when(z == 0)
     def _():
         for s in range(SUBS):
@@ -247,24 +252,64 @@
             value = c_all[ysize - 1, pl.ds(i, tall), :]
             for k in reversed(range(ysize - 1)):
                 value = times(value, wc.at[k], False)
-            tmp[pl.ds(i, tall), :] = value
+            cg[pl.ds(i, tall), :] = value
 
         tiles(width, tall, group_forward)
-        prepare(wp, tmp[:width, :width].T, -tmp[:width, width:].T)
+
+        @pl.when(lends)
+        def _():
+            remote(cg, dz, sem_one, 2, 2, behind).start()
+            remote(qg, rz, sem_one, 3, 3, behind).start()
+
+        @pl.when(jnp.logical_not(lends))
+        def _():
+            prepare(wp, cg[:, :width].T, -cg[:, width:].T)
+
+        @pl.when(skips)
+        def _():
+            prepare(wz1, cg[:, :width], cg[:, width:])
 
     early = z < 3
     pl.when(jnp.logical_not(early))(lambda: pass_on(d_all, sem_d))
 
+    @pl.when(skips)
+    def _():
+        remote(dz, dz, sem_one, 2, 2, ahead).wait_recv()
+
+        def joint(i):
+            tmp[pl.ds(i, tall), :] = times(dz[pl.ds(i, tall), :], wz1, False)
+
+        tiles(width, tall, joint)
+        prepare(wj, tmp[:width, :width].T, -tmp[:width, width:].T)
+        prepare(wq, dz[:, :width], dz[:, width:])
+        remote(rz, rz, sem_one, 3, 3, ahead).wait_recv()
+        rj[...] = times(qg[...], wq, True) + rz[...]
+
     for s in range(SUBS):
         rows = pl.ds(s * sub, sub)
 
-        @pl.when(z > 0)
+        @pl.when(jnp.logical_and(z > 0, jnp.logical_not(served)))
         def _():
             hop(vz, vz, sem_fz, s, behind).wait_recv()
 
-        @pl.when(jnp.logical_and(z > 0, z < zsize - 1))
+        @pl.when(served)
+        def _():
+            hop(vz, vz, sem_skip, s, two_back).wait_recv()
+
+        @pl.when(jnp.logical_and(jnp.logical_and(z > 0, z < zsize - 1), jnp.logical_not(jnp.logical_or(skips, lends))))
         def _():
             vo[rows, :] = times(vz[rows, :], wp, False) + qg[rows, :]
+            hop(vo, vz, sem_fz, s, ahead).start()
+
+        @pl.when(skips)
+        def _():
+            rj[rows, :] = times(vz[rows, :], wj, False) + rj[rows, :]
+            hop(rj, vz, sem_skip, s, two_on).start()
+
+    @pl.when(skips)
+    def _():
+        vo[...] = times(vz[...], wp, False) + qg[...]
+        for s in range(SUBS):
             hop(vo, vz, sem_fz, s, ahead).start()
 
     def hand_out(k, value, staging, into, sems):
@@ -297,7 +342,7 @@
         rows = pl.ds(pl.multiple_of(j * chunk, chunk), chunk)
         if d:
             remote(vin.at[rows, :], vin.at[rows, :], sem_v, j, j, {"y": j}).wait_recv()
-        ends = e0[rows, :] + times(vin[rows, :], wh, True)
+        ends = e0[rows, :] + times(vin[rows, :], wh, False)
         if d:
             eo[rows, :] = ends
             remote(eo.at[rows, :], e_all.at[y], sem_e, j, y, {"y": j}).start()
@@ -408,15 +453,14 @@
             def both(i):
                 rows = pl.ds(i, tall)
                 upper = jnp.concatenate([u_ref[0, 0, 0, rows, :], -u_ref[0, 0, 1, rows, :]], axis=1)
-                am[rows, :] = times(upper, wa1, False)
+                tmp[rows, :] = times(upper, wa1, False)
 
             tiles(width, tall, both)
-            prepare(wa0, am[:, :width], am[:, width:])
+            prepare(wa1, am[:, :width].T, -am[:, width:].T)
+            prepare(wa0, tmp[:width, :width].T, -tmp[:width, width:].T)
 
     soon = z >= zsize // 2
     pl.when(jnp.logical_not(soon))(settle)
-
-    two_on, two_back = along("z", z, 2, zsize), along("z", z, zsize - 2, zsize)
 
     def spread(s, k):
         rows = pl.ds(pl.multiple_of(y * chunk + s * sub, sub), sub)
@@ -498,8 +542,8 @@
                 inflow = wb[rows, :]
             else:
                 inflow = wz[...]
-            y1[rows, :] = y1[rows, :] - times(inflow, wa1, True)
-            y0[rows, :] = y0[rows, :] + times(inflow, wa0, True)
+            y1[rows, :] = y1[rows, :] - times(inflow, wa1, False)
+            y0[rows, :] = y0[rows, :] + times(inflow, wa0, False)
 
         for n, solved in enumerate((y0, y1)):
             real, imag = solved[rows, :width], solved[rows, width:]
@@ -618,9 +662,13 @@
         j, rows = rows_of(d)
         remote(eo.at[rows, :], e_all.at[y], sem_e, j, y, {"y": j}).wait_send()
     for s in range(SUBS):
-        @pl.when(z < zsize - 1)
+        @pl.when(jnp.logical_and(z < zsize - 1, jnp.logical_not(lends)))
         def _():
             hop(vo, vz, sem_fz, s, ahead).wait_send()
+
+        @pl.when(skips)
+        def _():
+            hop(rj, vz, sem_skip, s, two_on).wait_send()
 
         @pl.when(jnp.logical_or(last, jnp.logical_or(steps, jumps)))
         def _():
@@ -634,6 +682,11 @@
         def _():
             for d in order:
                 spread(s, lax.rem(y + d, ysize)).wait_send()
+
+    @pl.when(lends)
+    def _():
+        remote(cg, dz, sem_one, 2, 2, behind).wait_send()
+        remote(qg, rz, sem_one, 3, 3, behind).wait_send()
 
     @pl.when(feeds)
     def _():
@@ -676,7 +729,7 @@
         + [f32(ysize, chunk, wide)] * 2
         + [f32(chunk, wide)] * 4
         + [f32(vectors, wide)] * 10
-        + [f32(width, wide)] * 3
+        + [f32(width, wide)] * 4
         + [f32(chunk, wide)] * 4
         + [f32(ysize, chunk, wide)] * 2
         + [
@@ -699,7 +752,7 @@
         + [dma(ysize)] * 3
         + [dma(ysize * SUBS)]
         + [dma(SUBS)] * 2
-        + [dma(2), dma(SUBS)]
+        + [dma(4)] + [dma(SUBS)] * 2
         + [
             dma(ysize),
             dma(ysize * xsize),

time: 135 us -> 135 us (level)
  no operation moved by 1% of the time
where the time goes in v6:
time: 135 us
  Pallas kernels  133 us (99%)
  local copies, waits for them, and re-layouts  1.57 us (1%)
    pallas_call x1, Pallas kernels, shards(): pl.pallas_call(functools.partial(step_kernel, (xsize, zsize, ysize), tota...  133 us

profile of v6, /device:TPU:1, one launch (start us, length us, event | category | flops | bytes accessed | tf_op | source)
XLA Modules:
  0.0 134.8 jit_solution(18178372181099155659)
XLA Ops:
  0.0 133.2 %step.1 = f32[2,32,512]{2,1,0:T(8,128)} custom-call(f32[2,256,512]{2,1,0:T(8,128)} %f_hbm.1, f32[1,2,2,256,256]{4,3,2,1,0:T(8,128)} %g_hbm.1, f32[1,2,2,256,256]{4,3,2,1,0:T(8,128)} %e_hbm.1, f32[1,2,2,256,256]{4,3,2,1,0:T(8,128)} %u_hbm.1, f32[1,2]{1,0:T(1,128)} %w_ref.1), custom_call_target="tpu_custom_call" | custom-call | tf_op jit(solution)/shard_map/step/pallas_call | solution.py:718
  133.2 1.6 %copy.7 = f32[2,32,512]{2,1,0:T(8,128)} copy(f32[2,32,512]{2,1,0:T(8,128)} %step.1) | data formatting | bytes 262144

commit v7 on v5

--- a/solution.py
+++ b/solution.py
@@ -212,7 +212,7 @@
 
     tiles(width, tall, backward_map)
     pass_on(c_all, sem_c)
-    prepare(wh, tmp[:width, :width], tmp[:width, width:])
+    prepare(wh, tmp[:width, :width].T, -tmp[:width, width:].T)
 
     def local_ends(i):
         rows = pl.ds(i, tall)
@@ -297,7 +297,7 @@
         rows = pl.ds(pl.multiple_of(j * chunk, chunk), chunk)
         if d:
             remote(vin.at[rows, :], vin.at[rows, :], sem_v, j, j, {"y": j}).wait_recv()
-        ends = e0[rows, :] + times(vin[rows, :], wh, True)
+        ends = e0[rows, :] + times(vin[rows, :], wh, False)
         if d:
             eo[rows, :] = ends
             remote(eo.at[rows, :], e_all.at[y], sem_e, j, y, {"y": j}).start()
@@ -408,10 +408,11 @@
             def both(i):
                 rows = pl.ds(i, tall)
                 upper = jnp.concatenate([u_ref[0, 0, 0, rows, :], -u_ref[0, 0, 1, rows, :]], axis=1)
-                am[rows, :] = times(upper, wa1, False)
+                tmp[rows, :] = times(upper, wa1, False)
 
             tiles(width, tall, both)
-            prepare(wa0, am[:, :width], am[:, width:])
+            prepare(wa1, am[:, :width].T, -am[:, width:].T)
+            prepare(wa0, tmp[:width, :width].T, -tmp[:width, width:].T)
 
     soon = z >= zsize // 2
     pl.when(jnp.logical_not(soon))(settle)
@@ -498,17 +499,16 @@
                 inflow = wb[rows, :]
             else:
                 inflow = wz[...]
-            y1[rows, :] = y1[rows, :] - times(inflow, wa1, True)
-            y0[rows, :] = y0[rows, :] + times(inflow, wa0, True)
+            y1[rows, :] = y1[rows, :] - times(inflow, wa1, False)
+            y0[rows, :] = y0[rows, :] + times(inflow, wa0, False)
 
         for n, solved in enumerate((y0, y1)):
             real, imag = solved[rows, :width], solved[rows, width:]
             xs[n, rows, :width] = wreal * real - wimag * imag
             xs[n, rows, width:] = wreal * imag + wimag * real
         go(xs.at[1 - core, rows, :], other.at[rows, :], sem_a, turn, sibling)
-        if turn:
-            over_x(turn - 1, turns[turn - 1])
-    over_x(len(turns) - 1, turns[-1])
+        for done in {0: [0], 2: [1, 2]}.get(turn, [turn] if turn == len(turns) - 1 else []):
+            over_x(done, turns[done])
     for turn, d in enumerate(turns):
         _, rows = rows_of(d)
         for step in nearest_first(xsize):

time: 135 us -> 134 us (level)
  no operation moved by 1% of the time
where the time goes in v7:
time: 134 us
  Pallas kernels  132 us (99%)
  local copies, waits for them, and re-layouts  1.57 us (1%)
    pallas_call x1, Pallas kernels, shards(): pl.pallas_call(functools.partial(step_kernel, (xsize, zsize, ysize), tota...  132 us

profile of v7, /device:TPU:1, one launch (start us, length us, event | category | flops | bytes accessed | tf_op | source)
XLA Modules:
  0.0 133.9 jit_solution(3435606925664353048)
XLA Ops:
  0.0 132.3 %step.1 = f32[2,32,512]{2,1,0:T(8,128)} custom-call(f32[2,256,512]{2,1,0:T(8,128)} %f_hbm.1, f32[1,2,2,256,256]{4,3,2,1,0:T(8,128)} %g_hbm.1, f32[1,2,2,256,256]{4,3,2,1,0:T(8,128)} %e_hbm.1, f32[1,2,2,256,256]{4,3,2,1,0:T(8,128)} %u_hbm.1, f32[1,2]{1,0:T(1,128)} %w_ref.1), custom_call_target="tpu_custom_call" | custom-call | tf_op jit(solution)/shard_map/step/pallas_call | solution.py:665
  132.3 1.6 %copy.7 = f32[2,32,512]{2,1,0:T(8,128)} copy(f32[2,32,512]{2,1,0:T(8,128)} %step.1) | data formatting | bytes 262144

commit v8 on v7

--- a/solution.py
+++ b/solution.py
@@ -85,7 +85,7 @@
     vectors, width = f_ref.shape[1], g_ref.shape[-1]
     chunk = vectors // ysize
     sub = chunk // SUBS
-    tall = min(128, width)
+    tall = min(256, width)
     part = width // xsize
     own = vectors // poles
     line = own // ysize

time: 134 us -> 134 us (level)
  no operation moved by 1% of the time
where the time goes in v8:
time: 134 us
  Pallas kernels  132 us (99%)
  local copies, waits for them, and re-layouts  1.57 us (1%)
    pallas_call x1, Pallas kernels, shards(): pl.pallas_call(functools.partial(step_kernel, (xsize, zsize, ysize), tota...  132 us

profile of v8, /device:TPU:1, one launch (start us, length us, event | category | flops | bytes accessed | tf_op | source)
XLA Modules:
  0.0 133.9 jit_solution(13215469289716262501)
XLA Ops:
  0.0 132.3 %step.1 = f32[2,32,512]{2,1,0:T(8,128)} custom-call(f32[2,256,512]{2,1,0:T(8,128)} %f_hbm.1, f32[1,2,2,256,256]{4,3,2,1,0:T(8,128)} %g_hbm.1, f32[1,2,2,256,256]{4,3,2,1,0:T(8,128)} %e_hbm.1, f32[1,2,2,256,256]{4,3,2,1,0:T(8,128)} %u_hbm.1, f32[1,2]{1,0:T(1,128)} %w_ref.1), custom_call_target="tpu_custom_call" | custom-call | tf_op jit(solution)/shard_map/step/pallas_call | solution.py:665
  132.3 1.6 %copy.7 = f32[2,32,512]{2,1,0:T(8,128)} copy(f32[2,32,512]{2,1,0:T(8,128)} %step.1) | data formatting | bytes 262144

commit v9 on v8

--- a/solution.py
+++ b/solution.py
@@ -530,7 +530,7 @@
     rh, rl = halves(jnp.concatenate(right_side, axis=1))
     gram[...] = dot(lh, rh, True) + dot(ll, rh, True) + dot(lh, rl, True)
     plane = [(dx, dy) for dx in range(xsize) for dy in range(ysize) if dx or dy]
-    plane.sort(key=lambda p: min(p[0], xsize - p[0]) + min(p[1], ysize - p[1]))
+    plane.sort(key=lambda p: -min(p[0], xsize - p[0]) - min(p[1], ysize - p[1]))
     here = x * ysize + y
     for dx, dy in plane:
         slot = dx * ysize + dy
@@ -546,7 +546,7 @@
     for j in range(1, xsize * ysize):
         value = value + g1[j]
     g3[z] = value
-    for d in nearest_first(zsize):
+    for d in reversed(nearest_first(zsize)):
         go(g3.at[z], g3.at[z], sem_3, d, {"z": lax.rem(z + d, zsize)})
     for d in nearest_first(zsize):
         j = back(z, d, zsize)
@@ -557,6 +557,7 @@
     place = (core * xsize + x) * ysize + y
     lines(h1, place, line)[...] = value
     others = [(dp, dy) for dp in range(poles) for dy in range(ysize) if dp or dy]
+    others.sort(key=lambda p: -min(p[0], poles - p[0]) // 2 - min(p[1], ysize - p[1]))
     for dp, dy in others:
         device = pole_of(dp)[1] | along("y", y, dy, ysize)
         go(lines(h1, place, line), lines(h1, place, line), sem_5, dp * ysize + dy, device)

time: 134 us -> 133 us (level)
  no operation moved by 1% of the time
where the time goes in v9:
time: 133 us
  Pallas kernels  131 us (98%)
  local copies, waits for them, and re-layouts  1.57 us (1%)
    pallas_call x1, Pallas kernels, shards(): pl.pallas_call(functools.partial(step_kernel, (xsize, zsize, ysize), tota...  131 us

profile of v9, /device:TPU:1, one launch (start us, length us, event | category | flops | bytes accessed | tf_op | source)
XLA Modules:
  0.0 132.8 jit_solution(15464845640156771912)
XLA Ops:
  0.0 131.3 %step.1 = f32[2,32,512]{2,1,0:T(8,128)} custom-call(f32[2,256,512]{2,1,0:T(8,128)} %f_hbm.1, f32[1,2,2,256,256]{4,3,2,1,0:T(8,128)} %g_hbm.1, f32[1,2,2,256,256]{4,3,2,1,0:T(8,128)} %e_hbm.1, f32[1,2,2,256,256]{4,3,2,1,0:T(8,128)} %u_hbm.1, f32[1,2]{1,0:T(1,128)} %w_ref.1), custom_call_target="tpu_custom_call" | custom-call | tf_op jit(solution)/shard_map/step/pallas_call | solution.py:666
  131.3 1.6 %copy.7 = f32[2,32,512]{2,1,0:T(8,128)} copy(f32[2,32,512]{2,1,0:T(8,128)} %step.1) | data formatting | bytes 262144
